TPU v7x, 128 devices: a whole 4x4x4 slice. The times are simulated.
128 devices in a mesh: row: 8 (over x, y_lo), col: 16 (over z, y_hi, core).
Axes of the slice: x: 4, y: 4 (y_hi: 2, y_lo: 2; y = y_hi * 2 + y_lo), z: 4, core: 2. Of those that a mesh axis runs over, the one named last changes fastest.
Arguments:
- atom_blocks: float32 [128, 16, 128, 128], P('row', 'col'), may hold values from -6 to 6
- grid_position: int32 [128], replicated, may hold values from 0 to 127, as said below
- pattern: int32 [128, 16], replicated, may hold values from -1 to 127, as said below
Outputs:
- square: float32 [128, 16, 128, 128], P('row', 'col')
- update: float32 [128, 16, 128, 128], P('row', 'col')
Inputs may be any that keep to these rules, and one draw needn't show every extreme that they name: grid_position is a permutation; the 16 atom block rows a with a // 16 equal put at most 2 grid positions into any one run of 16 grid positions that starts at a multiple of 16, and exactly 2 into some run. `pattern`: each row holds 12 different block columns, one of them its own index, and -1 in its other slots; all slots s that hold one block column j have the same s; the block rows lie on a cycle of 128 places, not given, on which each row's columns lie within 16 places in a row around its own.
All inputs are finite; a program needn't handle non-finite values.
Results may differ from a plain program's by a relative error of at most 0.0003.
Values sent between devices are 32-bit elements; how exact they have to be, the bound alone decides.
No kernel may reach another device: no remote copies, remote signals or barrier semaphores. Data moves between devices by JAX's collectives and lax.ppermute only.
A program may use at most 128 MiB of HBM per device.

v0:
```python
import math

import jax
import jax.numpy as jnp
from jax import lax
from jax.sharding import PartitionSpec as P

NZ = 12


HIGHEST = lax.Precision.HIGHEST


def atoms_of_rows(grid_position, grid_rows):
    atom_numbers = jnp.arange(grid_position.shape[0], dtype=jnp.int32)
    hits = grid_position[None, :] == grid_rows[:, None]
    return jnp.sum(jnp.where(hits, atom_numbers[None, :], 0), axis=1)


def on_device(atom_blocks, grid_position, pattern):
    group_rows = atom_blocks.shape[0]
    local_slots = atom_blocks.shape[1]
    block_edge = atom_blocks.shape[2]
    row_count = lax.axis_size("row")
    row_index = lax.axis_index("row")
    column_index = lax.axis_index("col")
    local_rows = jnp.arange(group_rows, dtype=jnp.int32)
    grid_rows = row_index * group_rows + local_rows
    grid_atoms = atoms_of_rows(grid_position, grid_rows)
    capacity = 2 * ((group_rows + 2 * row_count - 1) // (2 * row_count))
    local_place = lax.dynamic_slice_in_dim(grid_position, row_index * group_rows, group_rows)
    target = local_place // group_rows
    ranking = jnp.sum(
        (target[None, :] == target[:, None]) & (local_rows[None, :] < local_rows[:, None]), axis=1
    )
    slot_code = target * capacity + ranking
    flat_slots = jnp.arange(row_count * capacity, dtype=jnp.int32)
    source = jnp.sum(
        jnp.where(slot_code[None, :] == flat_slots[:, None], local_rows[None, :], 0), axis=1
    )
    outgoing = jnp.take(atom_blocks, source, axis=0).reshape(
        row_count, capacity, local_slots, block_edge, block_edge
    )
    incoming = lax.all_to_all(outgoing, "row", split_axis=0, concat_axis=0, tiled=True)
    source_group = grid_atoms // group_rows
    within = grid_atoms % group_rows
    group_targets = (grid_position // group_rows).reshape(row_count, group_rows)
    their_targets = jnp.take(group_targets, source_group, axis=0)
    arrival = jnp.sum(
        (their_targets == row_index) & (local_rows[None, :] < within[:, None]), axis=1
    )
    slot_index = source_group * capacity + arrival
    arrived = incoming.reshape(row_count * capacity, local_slots, block_edge, block_edge)
    grid_blocks = jnp.take(arrived, slot_index, axis=0)
    grid_pattern = jnp.take(pattern, grid_atoms, axis=0)
    own_pattern = lax.dynamic_slice_in_dim(grid_pattern, column_index * local_slots, local_slots, 1)
    own_filled = own_pattern >= 0
    column_pattern = lax.dynamic_slice_in_dim(pattern, column_index * local_slots, local_slots, 1)
    start_scale = 1.0 / math.sqrt(NZ * block_edge)
    scale_back = math.sqrt(NZ * block_edge)
    matrix = jnp.where(own_filled[:, :, None, None], grid_blocks * start_scale, 0.0)

    def contribution(panel_part, right_panel):
        neighbours = jnp.maximum(grid_pattern, 0)
        right_rows = jnp.take(right_panel, jnp.take(grid_position, neighbours), axis=0)
        right_pattern = jnp.take(column_pattern, neighbours, axis=0)
        matches = (
            (right_pattern[:, :, :, None] == own_pattern[:, None, None, :])
            & own_filled[:, None, None, :]
            & (grid_pattern >= 0)[:, :, None, None]
        )
        weights = jnp.where(matches[:, :, 0, :, None, None], right_rows[:, :, 0][:, :, None], 0.0)
        return jnp.einsum("iupq,iutqr->itpr", panel_part, weights, precision=HIGHEST)

    def multiply(right_panel):
        return contribution(lax.all_gather(matrix, "col", axis=1, tiled=True), right_panel)

    right_panel = lax.all_gather(matrix, "row", axis=0, tiled=True)
    masked_square = multiply(right_panel)
    square_panel = lax.all_gather(masked_square, "row", axis=0, tiled=True)
    cubic = multiply(square_panel)
    square = masked_square * scale_back
    update = (1.5 * matrix - 0.5 * cubic) * scale_back
    return (square, update)


def solution(mesh):
    in_specs = (P("row", "col", None, None), P(), P())
    out_specs = (P("row", "col", None, None), P("row", "col", None, None))
    return jax.shard_map(
        on_device, mesh=mesh, in_specs=in_specs, out_specs=out_specs, check_vma=False
    )
```

profile of v0, /device:TPU:1, one launch (start us, length us, event | category | flops | bytes accessed | tf_op | source)
XLA Modules:
  0.0 573.4 jit_solution(7751069718583219607)
XLA Ops:
  7.2 0.9 select_reduce_fusion.1
  8.1 0.7 and_select_fusion.3
  8.9 0.2 convert_reduce_fusion.1
  9.1 0.7 multiply_add_fusion
  9.8 0.1 select_reduce_fusion
  10.0 0.6 gather_fusion.3
  10.6 1.1 bitcast_select_fusion.1
  11.7 5.9 %all-to-all-start = ((f32[8,2,1,128,128]{4,3,1,2,0:T(8,128)}), f32[8,2,1,128,128]{4,3,1,2,0:T(8,128)S(1)}, u32[]{:S(2)}, u32[]{:S(2)}) async-start(f32[8,2,1,128,128]{4,3,1,2,0:T(8,128)} %bitcast.5), calls=%async_computation | async-start | bytes 2097152 | tf_op jit(solution)/shard_map/all_to_all | solution.py:44
  17.6 0.7 and_select_fusion.1
  18.4 0.8 copy.41
  19.2 0.1 fusion.32
  19.4 0.6 gather_fusion.1
  19.9 0.6 gather_fusion
  20.6 0.2 compare_reduce_fusion
  20.8 0.2 convert_reduce_fusion
  21.0 11.8 %all-to-all-done = f32[8,2,1,128,128]{4,3,1,2,0:T(8,128)S(1)} async-done(((f32[8,2,1,128,128]{4,3,1,2,0:T(8,128)}), f32[8,2,1,128,128]{4,3,1,2,0:T(8,128)S(1)}, u32[]{:S(2)}, u32[]{:S(2)}) %all-to-all-start) | async-done | bytes 1048608 | tf_op jit(solution)/shard_map/all_to_all | solution.py:44
  32.7 0.6 gather_fusion.4
  33.4 1.2 fusion.31
  34.7 0.7 all-gather.6.cloned.1.call-update
  35.5 1.9 gather_fusion.5
  37.4 0.7 dynamic-slice_bitcast_fusion
  38.1 1.9 gather_fusion.2
  40.1 0.2 dynamic-slice_reduce_fusion
  40.5 163.5 %all-gather.4.cloned.1.call-done = f32[128,1,128,128]{3,2,1,0:T(8,128)} async-done(((f32[16,1,128,128]{3,2,1,0:T(8,128)}), f32[128,1,128,128]{3,2,1,0:T(8,128)}) %all-gather.4.cloned.1.call-update) | async-done | bytes 8388624 | tf_op jit(solution)/shard_map/all_gather | solution.py:78
  204.0 15.1 %gather_fusion.6 = f32[256,128,128]{2,1,0:T(8,128)} fusion(f32[128,128,128]{2,1,0:T(8,128)} %bitcast.69, s32[1024]{0:T(1024)S(1)} %pad_clamp_fusion), kind=kCustom, calls=%fused_computation.3.clone | custom fusion | bytes 33555456 | tf_op jit(solution)/shard_map/jit(_take)/gather | solution.py:65
  219.1 17.8 %copy.45 = f32[16,16,1,128,128]{3,4,1,0,2:T(8,128)} copy(f32[16,16,1,128,128]{4,3,1,0,2:T(8,128)} %bitcast.68) | data formatting | bytes 33554432 | tf_op jit(solution)/shard_map/jit(_take)/gather | solution.py:65
  236.9 85.3 %all-gather.6.cloned.1.call-done = f32[16,16,128,128]{3,2,1,0:T(8,128)} async-done(((f32[16,1,128,128]{3,2,1,0:T(8,128)}), f32[16,16,128,128]{3,2,1,0:T(8,128)}) %all-gather.6.cloned.1.call-update) | async-done | bytes 16777232 | tf_op jit(solution)/shard_map/all_gather | solution.py:76
  322.2 23.0 %broadcast_multiply_fusion = (f32[16,1,128,128]{3,2,1,0:T(8,128)}, f32[16,1,128,128]{3,2,1,0:T(8,128)}) fusion(f32[16,16,128,128]{3,2,1,0:T(8,128)} %all-gather.6.cloned.1.call-done, f32[16,16,1,128,128]{3,4,1,0,2:T(8,128)} %copy.45, pred[16,16]{1,0:T(8,128)(4,1)S(1)} %get-tuple-element.8, pred[16,16]{1,0:T(8,128)(4,1)S(1)} %get-tuple-element.16), kind=kOutput, calls=%fused_computation.32 | convolution fusion | flops 6451101696 | bytes 35652096 | tf_op jit(solution)/shard_map/iupq,iutqr->itpr/dot_general | solution.py:73
  345.3 165.6 %all-gather.8.cloned.1.call-done = f32[128,1,128,128]{3,2,1,0:T(8,128)} async-done(((f32[16,1,128,128]{3,2,1,0:T(8,128)}), f32[128,1,128,128]{3,2,1,0:T(8,128)}) %all-gather.8.cloned.1.call-update) | async-done | bytes 8388624 | tf_op jit(solution)/shard_map/all_gather | solution.py:80
  510.9 15.3 %gather_fusion.7 = f32[256,128,128]{2,1,0:T(8,128)} fusion(f32[128,128,128]{2,1,0:T(8,128)} %bitcast.70, s32[1024]{0:T(1024)S(1)} %pad_clamp_fusion), kind=kCustom, calls=%fused_computation.5.clone | custom fusion | bytes 33555456 | tf_op jit(solution)/shard_map/jit(_take)/gather | solution.py:65
  526.3 17.8 %copy.47 = f32[16,16,1,128,128]{3,4,1,0,2:T(8,128)} copy(f32[16,16,1,128,128]{4,3,1,0,2:T(8,128)} %bitcast.67) | data formatting | bytes 33554432 | tf_op jit(solution)/shard_map/jit(_take)/gather | solution.py:65
  544.0 22.8 %fusion.27 = f32[16,1,128,128]{3,2,1,0:T(8,128)} fusion(f32[16,16,128,128]{3,2,1,0:T(8,128)} %all-gather.6.cloned.1.call-done, f32[16,16,1,128,128]{3,4,1,0,2:T(8,128)} %copy.47, pred[16,16]{1,0:T(8,128)(4,1)S(1)} %get-tuple-element.8, pred[16,16]{1,0:T(8,128)(4,1)S(1)} %get-tuple-element.16, f32[16,1,128,128]{3,2,1,0:T(8,128)S(1)} %copy-done.3), kind=kOutput, calls=%fused_computation.27 | convolution fusion | flops 6451888128 | bytes 35652096 | tf_op jit(solution)/shard_map/iupq,iutqr->itpr/dot_general | solution.py:73
  (30 shorter events, 0.9 us)
Async XLA Ops:
  7.2 2.8 copy-start
  7.2 28.3 %copy-start.2 = (s32[128]{0:T(128)S(1)}, s32[128]{0:T(128)}, u32[]{:S(2)}) copy-start(s32[128]{0:T(128)} %param.12) | copy-start | bytes 1540
  11.7 21.0 %all-to-all-start = ((f32[8,2,1,128,128]{4,3,1,2,0:T(8,128)}), f32[8,2,1,128,128]{4,3,1,2,0:T(8,128)S(1)}, u32[]{:S(2)}, u32[]{:S(2)}) async-start(f32[8,2,1,128,128]{4,3,1,2,0:T(8,128)} %bitcast.5), calls=%async_computation | async-start | bytes 2097152 | tf_op jit(solution)/shard_map/all_to_all | solution.py:44
  17.6 186.4 %all-gather.4.cloned.1.call-start = ((), (), s32[]{:S(2)}) async-start(), calls=%async_computation.1 | async-start | bytes 9437184 | tf_op jit(solution)/shard_map/all_gather | solution.py:78
  34.6 287.6 %all-gather.6.cloned.1.call-start = ((), (), s32[]{:S(2)}) async-start(), calls=%async_computation.2 | async-start | bytes 17825792 | tf_op jit(solution)/shard_map/all_gather | solution.py:76
  35.4 475.6 %all-gather.8.cloned.1.call-start = ((), (), s32[]{:S(2)}) async-start(), calls=%async_computation.3 | async-start | bytes 9437184 | tf_op jit(solution)/shard_map/all_gather | solution.py:80
  526.2 17.8 %copy-start.3 = (f32[16,1,128,128]{3,2,1,0:T(8,128)S(1)}, f32[16,1,128,128]{3,2,1,0:T(8,128)}, u32[]{:S(2)}) copy-start(f32[16,1,128,128]{3,2,1,0:T(8,128)} %fusion.31) | copy-start | bytes 3145732
  526.3 40.6 %copy-start.1 = (f32[16,1,128,128]{3,2,1,0:T(8,128)S(1)}, f32[16,1,128,128]{3,2,1,0:T(8,128)}, u32[]{:S(2)}) copy-start(f32[16,1,128,128]{3,2,1,0:T(8,128)} %param.11) | copy-start | bytes 3145732
Sparse Core Ops, SparseCore 0:
  34.7 169.1 all-gather.3
  207.0 115.1 all-gather.5
  345.4 165.4 all-gather.7
where the time goes:
time: 578 us; the launch traced here: 573 us
  waiting for transfers between devices  427 us (74%)
  local copies, waits for them, and re-layouts  74.3 us (13%)
  matrix products  45.9 us (8%)
  between operations  13.9 us (2%)
  other arithmetic  6.41 us (1%)
  starting transfers between devices  5.98 us (1%)
    all_gather x1, waiting for transfers between devices, on_device(): square_panel = lax.all_gather(masked_square, 'row', axis=0, tiled=True)  166 us
    all_gather x1, waiting for transfers between devices, on_device(): right_panel = lax.all_gather(matrix, 'row', axis=0, tiled=True)  163 us
    all_gather x1, waiting for transfers between devices, multiply(): lax.all_gather(matrix, 'col', axis=1, tiled=True)  85.3 us
    gather x4, local copies, waits for them, and re-layouts, contribution(): jnp.take(right_panel, jnp.take(grid_position, neighbours), axis=0)  66.1 us
    dot_general x2, matrix products, contribution(): jnp.einsum('iupq,iutqr->itpr', panel_part, weights, precision=HIGHEST)  45.9 us
    all_to_all x1, waiting for transfers between devices, on_device(): lax.all_to_all(outgoing, 'row', split_axis=0, concat_axis=0, tiled=True)  11.8 us
  transfers between devices with their start and end apart: 4, of which 4 were waited for; matrix products, arithmetic and copies ran while one was open for 7% of the time, Pallas kernels for 0%

commit v1 on v0

v1 whole, which is shorter than its diff:
```python
import math

import jax
import jax.numpy as jnp
from jax import lax
from jax.experimental import pallas as pl
from jax.experimental.pallas import tpu as pltpu
from jax.sharding import PartitionSpec as P

AXES = ("row", "col")
NX, NYL, NZ_, NYH, NCORE = 4, 2, 4, 2, 2
ROWS = 16
SLOTS = 16
ATOMS = 128
EDGE = 128
HALF = 8


def _places():
    for x in range(NX):
        for yl in range(NYL):
            for z in range(NZ_):
                for yh in range(NYH):
                    for core in range(NCORE):
                        yield x, yl, z, yh, core


def _linear(x, yl, z, yh, core):
    return (x * NYL + yl) * (NZ_ * NYH * NCORE) + (z * NYH + yh) * NCORE + core


def _moves(step):
    return [(_linear(*p), _linear(*step(*p))) for p in _places()]


def _way(core):
    return 1 if core == 0 else -1


def _y_step(x, yl, z, yh, core):
    y = (yh * NYL + yl + _way(core)) % (NYL * NYH)
    return x, y % NYL, z, y // NYL, core


MOVE_XA = _moves(lambda x, yl, z, yh, c: ((x + _way(c)) % NX, yl, z, yh, c))
MOVE_XB = _moves(lambda x, yl, z, yh, c: ((x - _way(c)) % NX, yl, z, yh, c))
MOVE_YP = _moves(lambda x, yl, z, yh, c: (x, 1 - yl, z, yh, c))
MOVE_ZA = _moves(lambda x, yl, z, yh, c: (x, yl, (z + _way(c)) % NZ_, yh, c))
MOVE_ZB = _moves(lambda x, yl, z, yh, c: (x, yl, (z - _way(c)) % NZ_, yh, c))
MOVE_YA = _moves(_y_step)
MOVE_C = _moves(lambda x, yl, z, yh, c: (x, yl, z, yh, 1 - c))


def move(value, moves):
    return lax.ppermute(value, AXES, moves)


def after(value, *others):
    return lax.optimization_barrier((value, *others))[0]


def _split(value):
    high = value.astype(jnp.bfloat16)
    low = (value - high.astype(jnp.float32)).astype(jnp.bfloat16)
    return high, low


def _pick_kernel(table, *refs):
    n = len(refs) - 2
    pieces, out, sems = refs[:n], refs[n], refs[n + 1]
    copies = []
    for q in range(n):
        for s in range(2):
            e = q * 2 + s
            copies.append(
                pltpu.make_async_copy(
                    pieces[q].at[table[e]], out.at[table[2 * n + e]], sems.at[e]
                )
            )
    for c in copies:
        c.start()
    for c in copies:
        c.wait()


def pick_rows(pieces, table):
    n = len(pieces)
    return pl.pallas_call(
        _pick_kernel,
        out_shape=jax.ShapeDtypeStruct((2 * n, EDGE, EDGE), jnp.float32),
        in_specs=[pl.BlockSpec(memory_space=pltpu.SMEM)]
        + [pl.BlockSpec(memory_space=pltpu.HBM)] * n,
        out_specs=pl.BlockSpec(memory_space=pltpu.VMEM),
        scratch_shapes=[pltpu.SemaphoreType.DMA((2 * n,))],
        compiler_params=pltpu.CompilerParams(vmem_limit_bytes=VMEM_LIMIT),
        name="pick_rows",
    )(table, *pieces)


def _start_left(table, left, lbuf, lsem, base, rows):
    def row(local, carry):
        t = base + local
        for p in range(SLOTS):
            rank = table[t, p]

            @pl.when(rank >= 0)
            def _():
                pltpu.make_async_copy(
                    left[p].at[local], lbuf.at[t, rank], lsem.at[t, p]
                ).start()

        return carry

    lax.fori_loop(0, rows, row, 0)


def _product(table, lbuf, rpan, t, start, count):
    ls, rs = [], []
    for n in range(start, start + count):
        ls.append(lbuf[t, table[t, 2 * SLOTS + n]])
        rs.append(rpan[table[t, SLOTS + n]])
    lh, ll = _split(jnp.concatenate(ls, axis=1))
    rh, rl = _split(jnp.concatenate(rs, axis=0))
    four = jnp.dot(
        jnp.concatenate([lh, ll], axis=0),
        jnp.concatenate([rh, rl], axis=1),
        preferred_element_type=jnp.float32,
    )
    return (four[:EDGE, :EDGE] + (four[:EDGE, EDGE:] + four[EDGE:, :EDGE])) + four[
        EDGE:, EDGE:
    ]


def _row_product(table, lbuf, rpan, acc, t):
    total = table[t, 3 * SLOTS]

    @pl.when(total > 0)
    def _():
        acc[...] = _product(table, lbuf, rpan, t, 0, 8)

    @pl.when(total == 0)
    def _():
        acc[...] = jnp.zeros((EDGE, EDGE), jnp.float32)

    @pl.when(total > 8)
    def _():
        acc[...] += _product(table, lbuf, rpan, t, 8, 4)


def _wait_row(table, left, lbuf, lsem, t, local):
    for p in range(SLOTS):
        rank = table[t, p]

        @pl.when(rank >= 0)
        def _():
            pltpu.make_async_copy(
                left[p].at[local], lbuf.at[t, rank], lsem.at[t, p]
            ).wait()


def _square_kernel(scale, n_rows, table, *refs):
    left = refs[:SLOTS]
    right = refs[SLOTS : SLOTS + 8]
    out, lbuf, rpan, acc, lsem, rsem = refs[SLOTS + 8 :]
    per = right[0].shape[0]
    loads = [
        pltpu.make_async_copy(right[q], rpan.at[pl.ds(q * per, per)], rsem.at[q])
        for q in range(8)
    ]
    for c in loads:
        c.start()
    _start_left(table, left, lbuf, lsem, 0, n_rows)
    rpan[ATOMS] = jnp.zeros((EDGE, EDGE), jnp.float32)
    for c in loads:
        c.wait()

    def row(t, carry):
        _wait_row(table, left, lbuf, lsem, t, t)
        _row_product(table, lbuf, rpan, acc, t)
        out[t] = acc[...] * scale
        return carry

    lax.fori_loop(0, n_rows, row, 0)


MOST = 12
VMEM_LIMIT = 58 * 2**20


def square_rows(table, left, right, scale):
    n_rows = left[0].shape[0]
    return pl.pallas_call(
        lambda *refs: _square_kernel(scale, n_rows, *refs),
        out_shape=jax.ShapeDtypeStruct((n_rows, EDGE, EDGE), jnp.float32),
        in_specs=[pl.BlockSpec(memory_space=pltpu.SMEM)]
        + [pl.BlockSpec(memory_space=pltpu.HBM)] * (SLOTS + 8),
        out_specs=pl.BlockSpec(memory_space=pltpu.VMEM),
        scratch_shapes=[
            pltpu.VMEM((n_rows, MOST, EDGE, EDGE), jnp.float32),
            pltpu.VMEM((ATOMS + 1, EDGE, EDGE), jnp.float32),
            pltpu.VMEM((EDGE, EDGE), jnp.float32),
            pltpu.SemaphoreType.DMA((n_rows, SLOTS)),
            pltpu.SemaphoreType.DMA((8,)),
        ],
        compiler_params=pltpu.CompilerParams(vmem_limit_bytes=VMEM_LIMIT),
        name="square_rows",
    )(table, *left, *right)


def _update_kernel(scale, table, *refs):
    left_a = refs[:SLOTS]
    left_b = refs[SLOTS : 2 * SLOTS]
    right = refs[2 * SLOTS : 2 * SLOTS + 16]
    square, update, lbuf, rpan, acc, ubuf, lsem, rsem, ssem, usem = refs[2 * SLOTS + 16 :]
    loads = [
        pltpu.make_async_copy(right[q], rpan.at[pl.ds(q * HALF, HALF)], rsem.at[q])
        for q in range(16)
    ]
    for c in loads:
        c.start()
    _start_left(table, left_a, lbuf, lsem, 0, HALF)
    _start_left(table, left_b, lbuf, lsem, HALF, HALF)
    rpan[ATOMS] = jnp.zeros((EDGE, EDGE), jnp.float32)
    for c in loads:
        c.wait()
    squares = [
        pltpu.make_async_copy(
            rpan.at[64 * (t // HALF) + t % HALF],
            square.at[table[t, 3 * SLOTS + 1]],
            ssem.at[t],
        )
        for t in range(ROWS)
    ]
    for c in squares:
        c.start()

    def put(t):
        return pltpu.make_async_copy(
            ubuf.at[t], update.at[table[t, 3 * SLOTS + 1]], usem.at[t]
        )

    def rows(left, base):
        def row(local, carry):
            t = base + local
            _wait_row(table, left, lbuf, lsem, t, local)
            _row_product(table, lbuf, rpan, acc, t)
            filled = table[t, 3 * SLOTS] > 0
            ubuf[t] = jnp.where(
                filled, 1.5 * lbuf[t, 0] - (0.5 * scale) * acc[...], 0.0
            )
            put(t).start()
            return carry

        lax.fori_loop(0, HALF, row, 0)

    rows(left_a, 0)
    rows(left_b, HALF)
    for t in range(ROWS):
        put(t).wait()
    for c in squares:
        c.wait()


def update_rows(table, left_a, left_b, right, scale):
    out = jax.ShapeDtypeStruct((ROWS, EDGE, EDGE), jnp.float32)
    hbm = pl.BlockSpec(memory_space=pltpu.HBM)
    return pl.pallas_call(
        lambda *refs: _update_kernel(scale, *refs),
        out_shape=(out, out),
        in_specs=[pl.BlockSpec(memory_space=pltpu.SMEM)] + [hbm] * (2 * SLOTS + 16),
        out_specs=(hbm, hbm),
        scratch_shapes=[
            pltpu.VMEM((ROWS, MOST, EDGE, EDGE), jnp.float32),
            pltpu.VMEM((ATOMS + 1, EDGE, EDGE), jnp.float32),
            pltpu.VMEM((EDGE, EDGE), jnp.float32),
            pltpu.VMEM((ROWS, EDGE, EDGE), jnp.float32),
            pltpu.SemaphoreType.DMA((ROWS, SLOTS)),
            pltpu.SemaphoreType.DMA((16,)),
            pltpu.SemaphoreType.DMA((ROWS,)),
            pltpu.SemaphoreType.DMA((ROWS,)),
        ],
        compiler_params=pltpu.CompilerParams(vmem_limit_bytes=VMEM_LIMIT),
        name="update_rows",
    )(table, *left_a, *left_b, *right)


def _mod4(v):
    return v & 3


def _order(dx, dy):
    return jnp.where(
        dy == 0,
        jnp.where(dx == 0, 0, jnp.where(dx == 1, 1, jnp.where(dx == 3, 2, 6))),
        jnp.where(dx == 0, 3, jnp.where(dx == 1, 4, jnp.where(dx == 3, 5, 7))),
    )


def _piece(dx, dy, way):
    return _order(_mod4(-way * dx), dy)


def _lookup(keys, values):
    atoms = jnp.arange(ATOMS, dtype=jnp.int32)
    return jnp.sum(jnp.where(keys[..., None] == atoms, values, 0), axis=-1)


def build_tables(grid_position, pattern):
    i32 = jnp.int32
    row = lax.axis_index("row").astype(i32)
    col = lax.axis_index("col").astype(i32)
    x, yl = row // 2, row % 2
    z, yh, core = col // 4, (col // 2) % 2, col % 2
    way = 1 - 2 * core
    atoms = jnp.arange(ATOMS, dtype=i32)
    eights = jnp.arange(8, dtype=i32)
    sixteen = jnp.arange(16, dtype=i32)
    group = atoms // ROWS
    target = grid_position // ROWS
    same = (group[:, None] == group[None, :]) & (target[:, None] == target[None, :])
    rank = jnp.sum((same & (atoms[None, :] < atoms[:, None])).astype(i32), axis=1)
    place = 2 * _order(
        _mod4(group // 2 - target // 2), (group % 2) ^ (target % 2)
    ) + rank
    mine = target == row
    local_atom = jnp.sum(
        jnp.where(mine[None, :] & (place[None, :] == sixteen[:, None]), atoms[None, :], 0),
        axis=1,
    )
    source = _piece(_mod4(group // 2 - x), (group % 2) ^ yl, way)
    pick = 2 * source + rank
    hit = mine[None, :] & (pick[None, :] == sixteen[:, None])
    pick_row = jnp.sum(jnp.where(hit, (atoms % ROWS)[None, :], 0), axis=1)
    pick_place = jnp.sum(jnp.where(hit, place[None, :], 0), axis=1)
    pick_first = jnp.concatenate([pick_row[:HALF], pick_place[:HALF]])
    pick_rest = jnp.concatenate([pick_row[HALF:], pick_place[HALF:] - HALF])
    right_first = source * ROWS + atoms % ROWS
    holder = _piece(_mod4(target // 2 - x), (target % 2) ^ yl, way)
    right_second = (place // HALF) * 64 + holder * HALF + place % HALF
    def slots(d, c):
        dz = jnp.stack([0 * d, -d, d, 0 * d, -d, d, 0 * d + 2, 0 * d + 2])
        flip = jnp.where(((eights >= 3) & (eights <= 5)) | (eights == 7), 1, 0)
        return _mod4(z + dz) * 4 + (yh ^ flip) * 2 + c

    slot_of = jnp.concatenate([slots(way, core), slots(-way, 1 - core)])
    column = lax.dynamic_slice_in_dim(pattern, col, 1, 1)[:, 0]
    local_pattern = jnp.sum(
        jnp.where((local_atom[:, None] == atoms)[:, :, None], pattern[None], 0), axis=1
    )
    ordered = jnp.sum(
        jnp.where((slot_of[:, None] == sixteen)[None], local_pattern[:, None, :], 0),
        axis=2,
    )
    mine_column = ordered[:, :1]
    match = (ordered >= 0) & (mine_column >= 0) & (_lookup(ordered, column) == mine_column)
    counts = match.astype(i32)
    before = jnp.sum(
        jnp.where(sixteen[None, None, :] < sixteen[None, :, None], counts[:, None, :], 0),
        axis=2,
    )
    total = jnp.sum(counts, axis=1)
    ranks = jnp.where(match, before, -1)
    chosen = ranks[:, None, :] == sixteen[None, :, None]
    used = sixteen[None, :] < total[:, None]
    left_place = jnp.where(used, sixteen[None, :], 0)
    local_grid = _lookup(local_atom, grid_position) % ROWS

    def table(right):
        found = jnp.sum(jnp.where(chosen, _lookup(ordered, right)[:, None, :], 0), axis=2)
        right_place = jnp.where(used, found, ATOMS)
        tail = jnp.stack([total, local_grid], axis=1)
        return jnp.concatenate(
            [ranks, right_place, left_place, jnp.pad(tail, ((0, 0), (0, 14)))], axis=1
        )

    return pick_first, pick_rest, table(right_first), table(right_second)


def on_device(atom_blocks, grid_position, pattern):
    scale = 1.0 / math.sqrt(12 * EDGE)
    blocks = atom_blocks[:, 0]
    pick_first, pick_rest, first_table, second_table = build_tables(grid_position, pattern)
    a = move(blocks, MOVE_XA)
    b = move(blocks, MOVE_XB)
    w = move(blocks, MOVE_YP)
    aa = move(a, MOVE_XA)
    wa = move(w, MOVE_XA)
    wb = move(w, MOVE_XB)
    rows_a = pick_rows([blocks, a, b, w], pick_first)
    fa = move(rows_a, MOVE_ZA)
    fb = move(rows_a, MOVE_ZB)
    fy = move(rows_a, MOVE_YA)
    fc = move(rows_a, MOVE_C)
    fh = move(fy, MOVE_YA)
    faa = move(after(fa, fy), MOVE_ZA)
    waa = move(aa, MOVE_YP)
    fca = move(after(fa, fb), MOVE_C)
    fcb = move(fb, MOVE_C)
    fha = move(after(fh, aa), MOVE_ZA)
    fhb = move(after(fh, aa), MOVE_ZB)
    fcaa = move(faa, MOVE_C)
    fch = move(fh, MOVE_C)
    rows_b = pick_rows([wa, wb, aa, waa], pick_rest)
    sa = move(rows_b, MOVE_ZA)
    sb = move(rows_b, MOVE_ZB)
    sy = move(rows_b, MOVE_YA)
    sc = move(rows_b, MOVE_C)
    fhaa = move(after(fha, rows_b), MOVE_ZA)
    fcha = move(after(fha, rows_b), MOVE_C)
    fchb = move(fhb, MOVE_C)
    fchaa = move(fhaa, MOVE_C)
    left_a = [rows_a, fa, fb, fh, fha, fhb, faa, fhaa]
    left_a += [fc, fca, fcb, fch, fcha, fchb, fcaa, fchaa]
    right = [blocks, a, b, w, wa, wb, aa, waa]
    square_a = square_rows(after(first_table[:HALF], sc), left_a, right, scale)
    ga = move(square_a, MOVE_XA)
    gb = move(square_a, MOVE_XB)
    gw = move(square_a, MOVE_YP)
    sh = move(after(sy, square_a), MOVE_YA)
    saa = move(after(sa, square_a), MOVE_ZA)
    sca = move(after(sa, square_a), MOVE_C)
    scb = move(after(sb, square_a), MOVE_C)
    gaa = move(after(ga, sy, sa), MOVE_XA)
    gwa = move(after(gw, sy, sa, gb), MOVE_XA)
    gwb = move(after(gw, sy, sa, gb), MOVE_XB)
    sha = move(after(sh, gw, gb), MOVE_ZA)
    shb = move(after(sh, gw, gb), MOVE_ZB)
    sch = move(sh, MOVE_C)
    scaa = move(saa, MOVE_C)
    gwaa = move(after(gaa, sh), MOVE_YP)
    shaa = move(after(sha, gaa), MOVE_ZA)
    scha = move(after(sha, gaa), MOVE_C)
    schb = move(shb, MOVE_C)
    schaa = move(shaa, MOVE_C)
    left_b = [rows_b, sa, sb, sh, sha, shb, saa, shaa]
    left_b += [sc, sca, scb, sch, scha, schb, scaa, schaa]
    square_b = square_rows(first_table[HALF:], left_b, right, scale)
    ha = move(square_b, MOVE_XA)
    hb = move(square_b, MOVE_XB)
    hw = move(square_b, MOVE_YP)
    haa = move(after(ha, gwa, gwb), MOVE_XA)
    hwa = move(hw, MOVE_XA)
    hwb = move(hw, MOVE_XB)
    hwaa = move(haa, MOVE_YP)
    panel = [square_a, ga, gb, gw, gwa, gwb, gaa, gwaa]
    panel += [square_b, ha, hb, hw, hwa, hwb, haa, hwaa]
    square, update = update_rows(second_table, left_a, left_b, panel, scale)
    return square[:, None], update[:, None]


def solution(mesh):
    in_specs = (P("row", "col", None, None), P(), P())
    out_specs = (P("row", "col", None, None), P("row", "col", None, None))
    return jax.shard_map(
        on_device, mesh=mesh, in_specs=in_specs, out_specs=out_specs, check_vma=False
    )
```

time: 578 us -> 230 us (0.40)
  waiting for transfers between devices: 427 us -> 108 us
  local copies, waits for them, and re-layouts: 74.3 us -> 8.79 us
  starting transfers between devices: 5.98 us -> 66.2 us
  matrix products: 45.9 us -> 0 us
  Pallas kernels: 0 us -> 38 us
  between operations: 13.9 us -> 1.29 us
    all_gather x3 -> x0, waiting for transfers between devices: 414 us -> none  [the longest x1 166 us: on_device(): square_panel = lax.all_gather(masked_square, 'row', axis=0, tiled=True)]
    ppermute x0 -> x53, waiting for transfers between devices: none -> 108 us  [move(): return lax.ppermute(value, AXES, moves)]
    gather x12 -> x0, local copies, waits for them, and re-layouts: 72.3 us -> none  [the longest x4 66.1 us: contribution(): jnp.take(right_panel, jnp.take(grid_position, neighbours), axis=0)]
    ppermute x0 -> x53, starting transfers between devices: none -> 66.2 us  [move(): return lax.ppermute(value, AXES, moves)]
    dot_general x2 -> x0, matrix products: 45.9 us -> none  [contribution(): jnp.einsum('iupq,iutqr->itpr', panel_part, weights, precision=HIGHEST)]
    pallas_call x0 -> x5, Pallas kernels: none -> 38 us  [the longest x2 18.6 us: square_rows(): pl.pallas_call(lambda *refs: _square_kernel(scale, n_rows, *refs), out_sh...]
    all_to_all x1 -> x0, waiting for transfers between devices: 11.8 us -> none  [on_device(): lax.all_to_all(outgoing, 'row', split_axis=0, concat_axis=0, tiled=True)]
    unnamed x9 -> x84, local copies, waits for them, and re-layouts: 0.82 us -> 7.66 us
  transfers between devices with their start and end apart: 4 -> 53, of which waited for: 4 -> 21; matrix products, arithmetic and copies ran while one was open for 7% -> 3% of each run, Pallas kernels for 0% -> 10%
where the time goes in v1:
time: 230 us; the launch traced here: 228 us
  waiting for transfers between devices  108 us (47%)
  starting transfers between devices  66.2 us (29%)
  Pallas kernels  38 us (17%)
  local copies, waits for them, and re-layouts  8.79 us (4%)
  other arithmetic  5.85 us (3%)
    ppermute x53, waiting for transfers between devices, move(): return lax.ppermute(value, AXES, moves)  108 us
    ppermute x53, starting transfers between devices, move(): return lax.ppermute(value, AXES, moves)  66.2 us
    pallas_call x2, Pallas kernels, square_rows(): pl.pallas_call(lambda *refs: _square_kernel(scale, n_rows, *refs), out_sh...  18.6 us
    pallas_call x1, Pallas kernels, update_rows(): pl.pallas_call(lambda *refs: _update_kernel(scale, *refs), out_shape=(out...  14.1 us
    unnamed x84, local copies, waits for them, and re-layouts  7.66 us
    pallas_call x2, Pallas kernels, pick_rows(): pl.pallas_call(_pick_kernel, out_shape=jax.ShapeDtypeStruct((2 * n, EDGE,...  5.22 us
  transfers between devices with their start and end apart: 53, of which 21 were waited for; matrix products, arithmetic and copies ran while one was open for 3% of the time, Pallas kernels for 10%

profile of v1, /device:TPU:1, one launch (start us, length us, event | category | flops | bytes accessed | tf_op | source)
XLA Modules:
  0.0 228.3 jit_solution(12707387996547306268)
XLA Ops:
  6.1 23.1 %collective-permute-done.refs_1_.refs_18_ = f32[16,128,128]{2,1,0:T(8,128)S(1)} collective-permute-done((f32[16,128,128]{2,1,0:T(8,128)}, f32[16,128,128]{2,1,0:T(8,128)S(1)}, u32[]{:S(2)}, u32[]{:S(2)}) %collective-permute-start) | collective-permute-done | bytes 1048608 | tf_op jit(solution)/shard_map/ppermute | solution.py:55
  34.2 2.6 %pick_rows.2.refs_1_ = f32[8,128,128]{2,1,0:T(8,128)} custom-call(s32[16]{0:T(128)} %pad_add_fusion.2.table, f32[16,128,128]{2,1,0:T(8,128)} %bitcast.16, f32[16,128,128]{2,1,0:T(8,128)} %copy-done.2, f32[16,128,128]{2,1,0:T(8,128)} %copy-done.1, f32[16,128,128]{2,1,0:T(8,128)} %copy-done), custom_call_target="tpu_custom_call" | custom-call | tf_op jit(solution)/shard_map/pick_rows/pallas_call | solution.py:88
  38.8 3.8 %collective-permute-start.3 = (f32[8,128,128]{2,1,0:T(8,128)}, f32[8,128,128]{2,1,0:T(8,128)}, u32[]{:S(2)}, u32[]{:S(2)}) collective-permute-start(f32[8,128,128]{2,1,0:T(8,128)} %pick_rows.2.refs_1_), channel_id=1, source_target_pairs={{0,4},{1,13},{2,6},{3,15},{4,8},{5,1},{6,10},{7,3},{8,12},{9,5},{1... | collective-permute-start | bytes 1572872 | tf_op jit(solution)/shard_map/ppermute | solution.py:55
  42.5 2.7 %collective-permute-start.11 = (f32[16,128,128]{2,1,0:T(8,128)}, f32[16,128,128]{2,1,0:T(8,128)S(1)}, u32[]{:S(2)}, u32[]{:S(2)}) collective-permute-start(f32[16,128,128]{2,1,0:T(8,128)} %copy-done), channel_id=1, source_target_pairs={{0,32},{1,97},{2,34},{3,99},{4,36},{5,101},{6,38},{7,103},{8,40},{... | collective-permute-start | bytes 3145736 | tf_op jit(solution)/shard_map/ppermute | solution.py:55
  51.7 9.0 %collective-permute-done.6.refs_4_ = f32[8,128,128]{2,1,0:T(8,128)} collective-permute-done((f32[8,128,128]{2,1,0:T(8,128)}, f32[8,128,128]{2,1,0:T(8,128)}, u32[]{:S(2)}, u32[]{:S(2)}) %collective-permute-start.6) | collective-permute-done | bytes 524320 | tf_op jit(solution)/shard_map/ppermute | solution.py:55
  60.7 2.7 %collective-permute-start.15 = (f32[8,128,128]{2,1,0:T(8,128)}, f32[8,128,128]{2,1,0:T(8,128)}, u32[]{:S(2)}, u32[]{:S(2)}) collective-permute-start(f32[8,128,128]{2,1,0:T(8,128)} %pick_rows.2.refs_1_), channel_id=1, source_target_pairs={{0,1},{1,0},{2,3},{3,2},{4,5},{5,4},{6,7},{7,6},{8,9},{9,8},{10,11... | collective-permute-start | bytes 1572872 | tf_op jit(solution)/shard_map/ppermute | solution.py:55
  63.4 2.7 %collective-permute-start.10 = (f32[8,128,128]{2,1,0:T(8,128)}, f32[8,128,128]{2,1,0:T(8,128)}, u32[]{:S(2)}, u32[]{:S(2)}) collective-permute-start(f32[8,128,128]{2,1,0:T(8,128)} %collective-permute-done.3.refs_2_), channel_id=1, source_target_pairs={{0,4},{1,13},{2,6},{3,15},{4,8},{5,1},{6,10},{7,3},{8,12},{9,5},{1... | collective-permute-start | bytes 1572872 | tf_op jit(solution)/shard_map/ppermute | solution.py:55
  66.1 2.5 %collective-permute-done.12.refs_1_.refs_22_ = f32[16,128,128]{2,1,0:T(8,128)S(1)} collective-permute-done((f32[16,128,128]{2,1,0:T(8,128)}, f32[16,128,128]{2,1,0:T(8,128)S(1)}, u32[]{:S(2)}, u32[]{:S(2)}) %collective-permute-start.12) | collective-permute-done | bytes 1048608 | tf_op jit(solution)/shard_map/ppermute | solution.py:55
  70.4 9.2 %collective-permute-done.13.refs_3_.refs_24_ = f32[16,128,128]{2,1,0:T(8,128)S(1)} collective-permute-done((f32[16,128,128]{2,1,0:T(8,128)}, f32[16,128,128]{2,1,0:T(8,128)S(1)}, u32[]{:S(2)}, u32[]{:S(2)}) %collective-permute-start.13) | collective-permute-done | bytes 1048608 | tf_op jit(solution)/shard_map/ppermute | solution.py:55
  80.7 2.6 %pick_rows.3.refs_1_.refs_17_ = f32[8,128,128]{2,1,0:T(8,128)} custom-call(s32[16]{0:T(128)} %pad_add_fusion.3.table, f32[16,128,128]{2,1,0:T(8,128)} %copy-done.4, f32[16,128,128]{2,1,0:T(8,128)} %copy-done.3, f32[16,128,128]{2,1,0:T(8,128)} %collective-permute-done.7.refs_2_.refs_23_, f32[16,128,128]{2,1,0:T(8,128)} %copy-done.5), custom_call_target="tpu_custom_call" | custom-call | tf_op jit(solution)/shard_map/pick_rows/pallas_call | solution.py:88
  83.7 2.8 %collective-permute-start.18 = (f32[8,128,128]{2,1,0:T(8,128)}, f32[8,128,128]{2,1,0:T(8,128)S(1)}, u32[]{:S(2)}, u32[]{:S(2)}) collective-permute-start(f32[8,128,128]{2,1,0:T(8,128)} %collective-permute-done.6.refs_4_), channel_id=1, source_target_pairs={{0,1},{1,0},{2,3},{3,2},{4,5},{5,4},{6,7},{7,6},{8,9},{9,8},{10,11... | collective-permute-start | bytes 1572872 | tf_op jit(solution)/shard_map/ppermute | solution.py:55
  88.4 7.5 %collective-permute-done.9.refs_6_ = f32[8,128,128]{2,1,0:T(8,128)S(1)} collective-permute-done((f32[8,128,128]{2,1,0:T(8,128)}, f32[8,128,128]{2,1,0:T(8,128)S(1)}, u32[]{:S(2)}, u32[]{:S(2)}) %collective-permute-start.9) | collective-permute-done | bytes 524320 | tf_op jit(solution)/shard_map/ppermute | solution.py:55
  95.9 2.6 %collective-permute-start.20 = (f32[8,128,128]{2,1,0:T(8,128)S(1)}, f32[8,128,128]{2,1,0:T(8,128)S(1)}, u32[]{:S(2)}, u32[]{:S(2)}) collective-permute-start(f32[8,128,128]{2,1,0:T(8,128)S(1)} %collective-permute-done.9.refs_6_), channel_id=1, source_target_pairs={{0,1},{1,0},{2,3},{3,2},{4,5},{5,4},{6,7},{7,6},{8,9},{9,8},{10,11... | collective-permute-start | bytes 1572872 | tf_op jit(solution)/shard_map/ppermute | solution.py:55
  104.5 8.9 %square_rows.2.refs_33_ = f32[8,128,128]{2,1,0:T(8,128)} custom-call(s32[8,64]{1,0:T(8,128)} %get-tuple-element.22.refs_0_, f32[8,128,128]{2,1,0:T(8,128)} %pick_rows.2.refs_1_, f32[8,128,128]{2,1,0:T(8,128)} %collective-permute-done.3.refs_2_, f32[8,128,128]{2,1,0:T(8,128)} %collective-permute-done.4.refs_3_, ...), custom_call_target="tpu_custom_call" | custom-call | tf_op jit(solution)/shard_map/square_rows/pallas_call | solution.py:192
  116.4 2.9 %collective-permute-start.23 = (f32[8,128,128]{2,1,0:T(8,128)S(1)}, f32[8,128,128]{2,1,0:T(8,128)S(1)}, u32[]{:S(2)}, u32[]{:S(2)}) collective-permute-start(f32[8,128,128]{2,1,0:T(8,128)S(1)} %copy-done.6), channel_id=1, source_target_pairs={{0,4},{1,13},{2,6},{3,15},{4,8},{5,1},{6,10},{7,3},{8,12},{9,5},{1... | collective-permute-start | bytes 1572872 | tf_op jit(solution)/shard_map/ppermute | solution.py:55
  119.4 2.5 %collective-permute-start.33 = (f32[8,128,128]{2,1,0:T(8,128)}, f32[8,128,128]{2,1,0:T(8,128)S(1)}, u32[]{:S(2)}, u32[]{:S(2)}) collective-permute-start(f32[8,128,128]{2,1,0:T(8,128)} %square_rows.2.refs_33_), channel_id=1, source_target_pairs={{0,32},{1,97},{2,34},{3,99},{4,36},{5,101},{6,38},{7,103},{8,40},{... | collective-permute-start | bytes 1572872 | tf_op jit(solution)/shard_map/ppermute | solution.py:55
  123.9 4.9 %collective-permute-done.28.refs_36_ = f32[8,128,128]{2,1,0:T(8,128)} collective-permute-done((f32[8,128,128]{2,1,0:T(8,128)}, f32[8,128,128]{2,1,0:T(8,128)}, u32[]{:S(2)}, u32[]{:S(2)}) %collective-permute-start.28) | collective-permute-done | bytes 524320 | tf_op jit(solution)/shard_map/ppermute | solution.py:55
  128.8 6.1 %collective-permute-done.27.refs_4_.refs_20_ = f32[8,128,128]{2,1,0:T(8,128)S(1)} collective-permute-done((f32[8,128,128]{2,1,0:T(8,128)S(1)}, f32[8,128,128]{2,1,0:T(8,128)S(1)}, u32[]{:S(2)}, u32[]{:S(2)}) %collective-permute-start.27) | collective-permute-done | bytes 524320 | tf_op jit(solution)/shard_map/ppermute | solution.py:55
  135.0 2.7 %collective-permute-start.30 = (f32[8,128,128]{2,1,0:T(8,128)S(1)}, f32[8,128,128]{2,1,0:T(8,128)S(1)}, u32[]{:S(2)}, u32[]{:S(2)}) collective-permute-start(f32[8,128,128]{2,1,0:T(8,128)S(1)} %collective-permute-done.27.refs_4_.refs_20_), channel_id=1, source_target_pairs={{0,4},{1,13},{2,6},{3,15},{4,8},{5,1},{6,10},{7,3},{8,12},{9,5},{1... | collective-permute-start | bytes 1572872 | tf_op jit(solution)/shard_map/ppermute | solution.py:55
  140.1 3.7 %collective-permute-done.30.refs_5_.refs_21_ = f32[8,128,128]{2,1,0:T(8,128)S(1)} collective-permute-done((f32[8,128,128]{2,1,0:T(8,128)S(1)}, f32[8,128,128]{2,1,0:T(8,128)S(1)}, u32[]{:S(2)}, u32[]{:S(2)}) %collective-permute-start.30) | collective-permute-done | bytes 524320 | tf_op jit(solution)/shard_map/ppermute | solution.py:55
  143.8 2.3 %collective-permute-done.34.refs_39_ = f32[8,128,128]{2,1,0:T(8,128)S(1)} collective-permute-done((f32[8,128,128]{2,1,0:T(8,128)S(1)}, f32[8,128,128]{2,1,0:T(8,128)S(1)}, u32[]{:S(2)}, u32[]{:S(2)}) %collective-permute-start.34) | collective-permute-done | bytes 524320 | tf_op jit(solution)/shard_map/ppermute | solution.py:55
  147.3 4.0 %collective-permute-done.32.refs_7_.refs_23_ = f32[8,128,128]{2,1,0:T(8,128)S(1)} collective-permute-done((f32[8,128,128]{2,1,0:T(8,128)S(1)}, f32[8,128,128]{2,1,0:T(8,128)S(1)}, u32[]{:S(2)}, u32[]{:S(2)}) %collective-permute-start.32) | collective-permute-done | bytes 524320 | tf_op jit(solution)/shard_map/ppermute | solution.py:55
  152.1 7.6 %collective-permute-done.31.refs_6_.refs_22_ = f32[8,128,128]{2,1,0:T(8,128)S(1)} collective-permute-done((f32[8,128,128]{2,1,0:T(8,128)S(1)}, f32[8,128,128]{2,1,0:T(8,128)S(1)}, u32[]{:S(2)}, u32[]{:S(2)}) %collective-permute-start.31) | collective-permute-done | bytes 524320 | tf_op jit(solution)/shard_map/ppermute | solution.py:55
  166.3 9.7 %square_rows.3.refs_41_ = f32[8,128,128]{2,1,0:T(8,128)} custom-call(s32[8,64]{1,0:T(8,128)} %get-tuple-element.58.refs_0_, f32[8,128,128]{2,1,0:T(8,128)} %pick_rows.3.refs_1_.refs_17_, f32[8,128,128]{2,1,0:T(8,128)} %copy-done.17, f32[8,128,128]{2,1,0:T(8,128)} %copy-done.18, f32[8,128,128]{2,1,0:T(8,128)} %copy-done.16, f32[8,128,128]{2,1,0:T(8,128)} %copy-done.19, ...), custom_call_target="tpu_custom_call" | custom-call | tf_op jit(solution)/shard_map/square_rows/pallas_call | solution.py:192
  176.9 2.6 %collective-permute-start.48 = (f32[8,128,128]{2,1,0:T(8,128)}, f32[8,128,128]{2,1,0:T(8,128)S(1)}, u32[]{:S(2)}, u32[]{:S(2)}) collective-permute-start(f32[8,128,128]{2,1,0:T(8,128)} %square_rows.3.refs_41_), channel_id=1, source_target_pairs={{0,16},{1,17},{2,18},{3,19},{4,20},{5,21},{6,22},{7,23},{8,24},{9,... | collective-permute-start | bytes 1572872 | tf_op jit(solution)/shard_map/ppermute | solution.py:55
  179.6 5.1 %collective-permute-done.46.refs_42_ = f32[8,128,128]{2,1,0:T(8,128)S(1)} collective-permute-done((f32[8,128,128]{2,1,0:T(8,128)}, f32[8,128,128]{2,1,0:T(8,128)S(1)}, u32[]{:S(2)}, u32[]{:S(2)}) %collective-permute-start.46) | collective-permute-done | bytes 524320 | tf_op jit(solution)/shard_map/ppermute | solution.py:55
  186.4 2.6 %collective-permute-start.45 = (f32[8,128,128]{2,1,0:T(8,128)}, f32[8,128,128]{2,1,0:T(8,128)S(1)}, u32[]{:S(2)}, u32[]{:S(2)}) collective-permute-start(f32[8,128,128]{2,1,0:T(8,128)} %copy-done.31), channel_id=1, source_target_pairs={{0,16},{1,17},{2,18},{3,19},{4,20},{5,21},{6,22},{7,23},{8,24},{9,... | collective-permute-start | bytes 1572872 | tf_op jit(solution)/shard_map/ppermute | solution.py:55
  189.0 3.2 %collective-permute-done.48.refs_44_ = f32[8,128,128]{2,1,0:T(8,128)S(1)} collective-permute-done((f32[8,128,128]{2,1,0:T(8,128)}, f32[8,128,128]{2,1,0:T(8,128)S(1)}, u32[]{:S(2)}, u32[]{:S(2)}) %collective-permute-start.48) | collective-permute-done | bytes 524320 | tf_op jit(solution)/shard_map/ppermute | solution.py:55
  194.9 3.2 %collective-permute-start.52 = (f32[8,128,128]{2,1,0:T(8,128)S(1)}, f32[8,128,128]{2,1,0:T(8,128)S(1)}, u32[]{:S(2)}, u32[]{:S(2)}) collective-permute-start(f32[8,128,128]{2,1,0:T(8,128)S(1)} %collective-permute-done.51.refs_47_), channel_id=1, source_target_pairs={{0,16},{1,17},{2,18},{3,19},{4,20},{5,21},{6,22},{7,23},{8,24},{9,... | collective-permute-start | bytes 1572872 | tf_op jit(solution)/shard_map/ppermute | solution.py:55
  198.1 4.9 %collective-permute-done.45.refs_40_ = f32[8,128,128]{2,1,0:T(8,128)S(1)} collective-permute-done((f32[8,128,128]{2,1,0:T(8,128)}, f32[8,128,128]{2,1,0:T(8,128)S(1)}, u32[]{:S(2)}, u32[]{:S(2)}) %collective-permute-start.45) | collective-permute-done | bytes 524320 | tf_op jit(solution)/shard_map/ppermute | solution.py:55
  204.4 8.4 %collective-permute-done.50.refs_46_ = f32[8,128,128]{2,1,0:T(8,128)S(1)} collective-permute-done((f32[8,128,128]{2,1,0:T(8,128)S(1)}, f32[8,128,128]{2,1,0:T(8,128)S(1)}, u32[]{:S(2)}, u32[]{:S(2)}) %collective-permute-start.50) | collective-permute-done | bytes 524320 | tf_op jit(solution)/shard_map/ppermute | solution.py:55
  214.0 14.1 %update_rows.1 = (f32[16,128,128]{2,1,0:T(8,128)}, f32[16,128,128]{2,1,0:T(8,128)}) custom-call(s32[16,64]{1,0:T(8,128)} %get-tuple-element.57.refs_0_, f32[8,128,128]{2,1,0:T(8,128)} %pick_rows.2.refs_1_, f32[8,128,128]{2,1,0:T(8,128)} %collective-permute-done.3.refs_2_, f32[8,128,128]{2,1,0:T(8,128)} %collective-permute-done.4.refs_3_, ...), custom_call_target="tpu_custom_call" | custom-call | tf_op jit(solution)/shard_map/update_rows/pallas_call | solution.py:267
  (201 shorter events, 53.7 us)
Async XLA Ops:
  0.6 31.6 %collective-permute-start.2 = (f32[16,128,128]{2,1,0:T(8,128)}, f32[16,128,128]{2,1,0:T(8,128)S(1)}, u32[]{:S(2)}, u32[]{:S(2)}) collective-permute-start(f32[16,128,128]{2,1,0:T(8,128)} %bitcast.13), channel_id=1, source_target_pairs={{0,16},{1,17},{2,18},{3,19},{4,20},{5,21},{6,22},{7,23},{8,24},{9,... | collective-permute-start | bytes 3145736 | tf_op jit(solution)/shard_map/ppermute | solution.py:55
  2.8 29.4 %collective-permute-start.1 = (f32[16,128,128]{2,1,0:T(8,128)}, f32[16,128,128]{2,1,0:T(8,128)S(1)}, u32[]{:S(2)}, u32[]{:S(2)}) collective-permute-start(f32[16,128,128]{2,1,0:T(8,128)} %bitcast.14), channel_id=1, source_target_pairs={{0,96},{1,33},{2,98},{3,35},{4,100},{5,37},{6,102},{7,39},{8,104},... | collective-permute-start | bytes 3145736 | tf_op jit(solution)/shard_map/ppermute | solution.py:55
  4.1 25.2 %collective-permute-start = (f32[16,128,128]{2,1,0:T(8,128)}, f32[16,128,128]{2,1,0:T(8,128)S(1)}, u32[]{:S(2)}, u32[]{:S(2)}) collective-permute-start(f32[16,128,128]{2,1,0:T(8,128)} %bitcast.15), channel_id=1, source_target_pairs={{0,32},{1,97},{2,34},{3,99},{4,36},{5,101},{6,38},{7,103},{8,40},{... | collective-permute-start | bytes 3145736 | tf_op jit(solution)/shard_map/ppermute | solution.py:55
  29.2 21.0 %collective-permute-start.7 = (f32[16,128,128]{2,1,0:T(8,128)S(1)}, f32[16,128,128]{2,1,0:T(8,128)}, u32[]{:S(2)}, u32[]{:S(2)}) collective-permute-start(f32[16,128,128]{2,1,0:T(8,128)S(1)} %collective-permute-done.refs_1_.refs_18_), channel_id=1, source_target_pairs={{0,32},{1,97},{2,34},{3,99},{4,36},{5,101},{6,38},{7,103},{8,40},{... | collective-permute-start | bytes 3145736 | tf_op jit(solution)/shard_map/ppermute | solution.py:55
  42.5 26.1 %collective-permute-start.12 = (f32[16,128,128]{2,1,0:T(8,128)}, f32[16,128,128]{2,1,0:T(8,128)S(1)}, u32[]{:S(2)}, u32[]{:S(2)}) collective-permute-start(f32[16,128,128]{2,1,0:T(8,128)} %copy-done), channel_id=1, source_target_pairs={{0,96},{1,33},{2,98},{3,35},{4,100},{5,37},{6,102},{7,39},{8,104},... | collective-permute-start | bytes 3145736 | tf_op jit(solution)/shard_map/ppermute | solution.py:55
  42.5 26.1 %collective-permute-start.11 = (f32[16,128,128]{2,1,0:T(8,128)}, f32[16,128,128]{2,1,0:T(8,128)S(1)}, u32[]{:S(2)}, u32[]{:S(2)}) collective-permute-start(f32[16,128,128]{2,1,0:T(8,128)} %copy-done), channel_id=1, source_target_pairs={{0,32},{1,97},{2,34},{3,99},{4,36},{5,101},{6,38},{7,103},{8,40},{... | collective-permute-start | bytes 3145736 | tf_op jit(solution)/shard_map/ppermute | solution.py:55
  45.8 17.6 %collective-permute-start.4 = (f32[8,128,128]{2,1,0:T(8,128)}, f32[8,128,128]{2,1,0:T(8,128)}, u32[]{:S(2)}, u32[]{:S(2)}) collective-permute-start(f32[8,128,128]{2,1,0:T(8,128)} %pick_rows.2.refs_1_), channel_id=1, source_target_pairs={{0,12},{1,5},{2,14},{3,7},{4,0},{5,9},{6,2},{7,11},{8,4},{9,13},{1... | collective-permute-start | bytes 1572872 | tf_op jit(solution)/shard_map/ppermute | solution.py:55
  50.2 29.4 %collective-permute-start.13 = (f32[16,128,128]{2,1,0:T(8,128)}, f32[16,128,128]{2,1,0:T(8,128)S(1)}, u32[]{:S(2)}, u32[]{:S(2)}) collective-permute-start(f32[16,128,128]{2,1,0:T(8,128)} %collective-permute-done.7.refs_2_.refs_23_), channel_id=1, source_target_pairs={{0,16},{1,17},{2,18},{3,19},{4,20},{5,21},{6,22},{7,23},{8,24},{9,... | collective-permute-start | bytes 3145736 | tf_op jit(solution)/shard_map/ppermute | solution.py:55
  60.7 23.0 %collective-permute-start.15 = (f32[8,128,128]{2,1,0:T(8,128)}, f32[8,128,128]{2,1,0:T(8,128)}, u32[]{:S(2)}, u32[]{:S(2)}) collective-permute-start(f32[8,128,128]{2,1,0:T(8,128)} %pick_rows.2.refs_1_), channel_id=1, source_target_pairs={{0,1},{1,0},{2,3},{3,2},{4,5},{5,4},{6,7},{7,6},{8,9},{9,8},{10,11... | collective-permute-start | bytes 1572872 | tf_op jit(solution)/shard_map/ppermute | solution.py:55
  63.4 23.1 %collective-permute-start.10 = (f32[8,128,128]{2,1,0:T(8,128)}, f32[8,128,128]{2,1,0:T(8,128)}, u32[]{:S(2)}, u32[]{:S(2)}) collective-permute-start(f32[8,128,128]{2,1,0:T(8,128)} %collective-permute-done.3.refs_2_), channel_id=1, source_target_pairs={{0,4},{1,13},{2,6},{3,15},{4,8},{5,1},{6,10},{7,3},{8,12},{9,5},{1... | collective-permute-start | bytes 1572872 | tf_op jit(solution)/shard_map/ppermute | solution.py:55
  68.6 17.9 %collective-permute-start.17 = (f32[8,128,128]{2,1,0:T(8,128)}, f32[8,128,128]{2,1,0:T(8,128)}, u32[]{:S(2)}, u32[]{:S(2)}) collective-permute-start(f32[8,128,128]{2,1,0:T(8,128)} %collective-permute-done.4.refs_3_), channel_id=1, source_target_pairs={{0,1},{1,0},{2,3},{3,2},{4,5},{5,4},{6,7},{7,6},{8,9},{9,8},{10,11... | collective-permute-start | bytes 1572872 | tf_op jit(solution)/shard_map/ppermute | solution.py:55
  68.6 14.7 %collective-permute-start.8 = (f32[8,128,128]{2,1,0:T(8,128)}, f32[8,128,128]{2,1,0:T(8,128)}, u32[]{:S(2)}, u32[]{:S(2)}) collective-permute-start(f32[8,128,128]{2,1,0:T(8,128)} %collective-permute-done.6.refs_4_), channel_id=1, source_target_pairs={{0,4},{1,13},{2,6},{3,15},{4,8},{5,1},{6,10},{7,3},{8,12},{9,5},{1... | collective-permute-start | bytes 1572872 | tf_op jit(solution)/shard_map/ppermute | solution.py:55
  83.7 14.8 %collective-permute-start.18 = (f32[8,128,128]{2,1,0:T(8,128)}, f32[8,128,128]{2,1,0:T(8,128)S(1)}, u32[]{:S(2)}, u32[]{:S(2)}) collective-permute-start(f32[8,128,128]{2,1,0:T(8,128)} %collective-permute-done.6.refs_4_), channel_id=1, source_target_pairs={{0,1},{1,0},{2,3},{3,2},{4,5},{5,4},{6,7},{7,6},{8,9},{9,8},{10,11... | collective-permute-start | bytes 1572872 | tf_op jit(solution)/shard_map/ppermute | solution.py:55
  86.5 14.4 %collective-permute-start.26 = (f32[8,128,128]{2,1,0:T(8,128)}, f32[8,128,128]{2,1,0:T(8,128)S(1)}, u32[]{:S(2)}, u32[]{:S(2)}) collective-permute-start(f32[8,128,128]{2,1,0:T(8,128)} %pick_rows.3.refs_1_.refs_17_), channel_id=1, source_target_pairs={{0,1},{1,0},{2,3},{3,2},{4,5},{5,4},{6,7},{7,6},{8,9},{9,8},{10,11... | collective-permute-start | bytes 1572872 | tf_op jit(solution)/shard_map/ppermute | solution.py:55
  88.3 14.2 %collective-permute-start.21 = (f32[8,128,128]{2,1,0:T(8,128)}, f32[8,128,128]{2,1,0:T(8,128)S(1)}, u32[]{:S(2)}, u32[]{:S(2)}) collective-permute-start(f32[8,128,128]{2,1,0:T(8,128)} %collective-permute-done.10.refs_7_), channel_id=1, source_target_pairs={{0,1},{1,0},{2,3},{3,2},{4,5},{5,4},{6,7},{7,6},{8,9},{9,8},{10,11... | collective-permute-start | bytes 1572872 | tf_op jit(solution)/shard_map/ppermute | solution.py:55
  98.7 16.8 %collective-permute-start.25 = (f32[8,128,128]{2,1,0:T(8,128)}, f32[8,128,128]{2,1,0:T(8,128)S(1)}, u32[]{:S(2)}, u32[]{:S(2)}) collective-permute-start(f32[8,128,128]{2,1,0:T(8,128)} %pick_rows.3.refs_1_.refs_17_), channel_id=1, source_target_pairs={{0,16},{1,19},{2,18},{3,17},{4,20},{5,23},{6,22},{7,21},{8,24},{9,... | collective-permute-start | bytes 1572872 | tf_op jit(solution)/shard_map/ppermute | solution.py:55
  115.5 13.3 %collective-permute-start.28 = (f32[8,128,128]{2,1,0:T(8,128)}, f32[8,128,128]{2,1,0:T(8,128)}, u32[]{:S(2)}, u32[]{:S(2)}) collective-permute-start(f32[8,128,128]{2,1,0:T(8,128)} %square_rows.2.refs_33_), channel_id=1, source_target_pairs={{0,16},{1,17},{2,18},{3,19},{4,20},{5,21},{6,22},{7,23},{8,24},{9,... | collective-permute-start | bytes 1572872 | tf_op jit(solution)/shard_map/ppermute | solution.py:55
  115.5 19.5 %collective-permute-start.27 = (f32[8,128,128]{2,1,0:T(8,128)S(1)}, f32[8,128,128]{2,1,0:T(8,128)S(1)}, u32[]{:S(2)}, u32[]{:S(2)}) collective-permute-start(f32[8,128,128]{2,1,0:T(8,128)S(1)} %collective-permute-done.25), channel_id=1, source_target_pairs={{0,16},{1,19},{2,18},{3,17},{4,20},{5,23},{6,22},{7,21},{8,24},{9,... | collective-permute-start | bytes 1572872 | tf_op jit(solution)/shard_map/ppermute | solution.py:55
  116.4 21.2 %collective-permute-start.23 = (f32[8,128,128]{2,1,0:T(8,128)S(1)}, f32[8,128,128]{2,1,0:T(8,128)S(1)}, u32[]{:S(2)}, u32[]{:S(2)}) collective-permute-start(f32[8,128,128]{2,1,0:T(8,128)S(1)} %copy-done.6), channel_id=1, source_target_pairs={{0,4},{1,13},{2,6},{3,15},{4,8},{5,1},{6,10},{7,3},{8,12},{9,5},{1... | collective-permute-start | bytes 1572872 | tf_op jit(solution)/shard_map/ppermute | solution.py:55
  119.4 18.3 %collective-permute-start.33 = (f32[8,128,128]{2,1,0:T(8,128)}, f32[8,128,128]{2,1,0:T(8,128)S(1)}, u32[]{:S(2)}, u32[]{:S(2)}) collective-permute-start(f32[8,128,128]{2,1,0:T(8,128)} %square_rows.2.refs_33_), channel_id=1, source_target_pairs={{0,32},{1,97},{2,34},{3,99},{4,36},{5,101},{6,38},{7,103},{8,40},{... | collective-permute-start | bytes 1572872 | tf_op jit(solution)/shard_map/ppermute | solution.py:55
  123.9 15.5 %collective-permute-start.24 = (f32[8,128,128]{2,1,0:T(8,128)S(1)}, f32[8,128,128]{2,1,0:T(8,128)S(1)}, u32[]{:S(2)}, u32[]{:S(2)}) collective-permute-start(f32[8,128,128]{2,1,0:T(8,128)S(1)} %copy-done.6), channel_id=1, source_target_pairs={{0,12},{1,5},{2,14},{3,7},{4,0},{5,9},{6,2},{7,11},{8,4},{9,13},{1... | collective-permute-start | bytes 1572872 | tf_op jit(solution)/shard_map/ppermute | solution.py:55
  143.8 16.0 %collective-permute-start.31 = (f32[8,128,128]{2,1,0:T(8,128)S(1)}, f32[8,128,128]{2,1,0:T(8,128)S(1)}, u32[]{:S(2)}, u32[]{:S(2)}) collective-permute-start(f32[8,128,128]{2,1,0:T(8,128)S(1)} %collective-permute-done.27.refs_4_.refs_20_), channel_id=1, source_target_pairs={{0,12},{1,5},{2,14},{3,7},{4,0},{5,9},{6,2},{7,11},{8,4},{9,13},{1... | collective-permute-start | bytes 1572872 | tf_op jit(solution)/shard_map/ppermute | solution.py:55
  146.1 14.6 %collective-permute-start.35 = (f32[8,128,128]{2,1,0:T(8,128)S(1)}, f32[8,128,128]{2,1,0:T(8,128)S(1)}, u32[]{:S(2)}, u32[]{:S(2)}) collective-permute-start(f32[8,128,128]{2,1,0:T(8,128)S(1)} %collective-permute-done.30.refs_5_.refs_21_), channel_id=1, source_target_pairs={{0,4},{1,13},{2,6},{3,15},{4,8},{5,1},{6,10},{7,3},{8,12},{9,5},{1... | collective-permute-start | bytes 1572872 | tf_op jit(solution)/shard_map/ppermute | solution.py:55
  147.3 14.4 %collective-permute-start.38 = (f32[8,128,128]{2,1,0:T(8,128)S(1)}, f32[8,128,128]{2,1,0:T(8,128)S(1)}, u32[]{:S(2)}, u32[]{:S(2)}) collective-permute-start(f32[8,128,128]{2,1,0:T(8,128)S(1)} %collective-permute-done.27.refs_4_.refs_20_), channel_id=1, source_target_pairs={{0,1},{1,0},{2,3},{3,2},{4,5},{5,4},{6,7},{7,6},{8,9},{9,8},{10,11... | collective-permute-start | bytes 1572872 | tf_op jit(solution)/shard_map/ppermute | solution.py:55
  161.7 17.9 %collective-permute-start.44 = (f32[8,128,128]{2,1,0:T(8,128)}, f32[8,128,128]{2,1,0:T(8,128)}, u32[]{:S(2)}, u32[]{:S(2)}) collective-permute-start(f32[8,128,128]{2,1,0:T(8,128)} %collective-permute-done.28.refs_36_), channel_id=1, source_target_pairs={{0,96},{1,33},{2,98},{3,35},{4,100},{5,37},{6,102},{7,39},{8,104},... | collective-permute-start | bytes 1572872 | tf_op jit(solution)/shard_map/ppermute | solution.py:55
  162.2 17.4 %collective-permute-start.43 = (f32[8,128,128]{2,1,0:T(8,128)}, f32[8,128,128]{2,1,0:T(8,128)}, u32[]{:S(2)}, u32[]{:S(2)}) collective-permute-start(f32[8,128,128]{2,1,0:T(8,128)} %collective-permute-done.28.refs_36_), channel_id=1, source_target_pairs={{0,32},{1,97},{2,34},{3,99},{4,36},{5,101},{6,38},{7,103},{8,40},{... | collective-permute-start | bytes 1572872 | tf_op jit(solution)/shard_map/ppermute | solution.py:55
  176.9 15.3 %collective-permute-start.48 = (f32[8,128,128]{2,1,0:T(8,128)}, f32[8,128,128]{2,1,0:T(8,128)S(1)}, u32[]{:S(2)}, u32[]{:S(2)}) collective-permute-start(f32[8,128,128]{2,1,0:T(8,128)} %square_rows.3.refs_41_), channel_id=1, source_target_pairs={{0,16},{1,17},{2,18},{3,19},{4,20},{5,21},{6,22},{7,23},{8,24},{9,... | collective-permute-start | bytes 1572872 | tf_op jit(solution)/shard_map/ppermute | solution.py:55
  186.4 16.6 %collective-permute-start.45 = (f32[8,128,128]{2,1,0:T(8,128)}, f32[8,128,128]{2,1,0:T(8,128)S(1)}, u32[]{:S(2)}, u32[]{:S(2)}) collective-permute-start(f32[8,128,128]{2,1,0:T(8,128)} %copy-done.31), channel_id=1, source_target_pairs={{0,16},{1,17},{2,18},{3,19},{4,20},{5,21},{6,22},{7,23},{8,24},{9,... | collective-permute-start | bytes 1572872 | tf_op jit(solution)/shard_map/ppermute | solution.py:55
  189.0 15.4 %collective-permute-start.47 = (f32[8,128,128]{2,1,0:T(8,128)}, f32[8,128,128]{2,1,0:T(8,128)S(1)}, u32[]{:S(2)}, u32[]{:S(2)}) collective-permute-start(f32[8,128,128]{2,1,0:T(8,128)} %square_rows.3.refs_41_), channel_id=1, source_target_pairs={{0,96},{1,33},{2,98},{3,35},{4,100},{5,37},{6,102},{7,39},{8,104},... | collective-permute-start | bytes 1572872 | tf_op jit(solution)/shard_map/ppermute | solution.py:55
  192.2 20.6 %collective-permute-start.50 = (f32[8,128,128]{2,1,0:T(8,128)S(1)}, f32[8,128,128]{2,1,0:T(8,128)S(1)}, u32[]{:S(2)}, u32[]{:S(2)}) collective-permute-start(f32[8,128,128]{2,1,0:T(8,128)S(1)} %collective-permute-done.48.refs_44_), channel_id=1, source_target_pairs={{0,96},{1,33},{2,98},{3,35},{4,100},{5,37},{6,102},{7,39},{8,104},... | collective-permute-start | bytes 1572872 | tf_op jit(solution)/shard_map/ppermute | solution.py:55
  192.7 20.1 %collective-permute-start.49 = (f32[8,128,128]{2,1,0:T(8,128)S(1)}, f32[8,128,128]{2,1,0:T(8,128)S(1)}, u32[]{:S(2)}, u32[]{:S(2)}) collective-permute-start(f32[8,128,128]{2,1,0:T(8,128)S(1)} %collective-permute-done.48.refs_44_), channel_id=1, source_target_pairs={{0,32},{1,97},{2,34},{3,99},{4,36},{5,101},{6,38},{7,103},{8,40},{... | collective-permute-start | bytes 1572872 | tf_op jit(solution)/shard_map/ppermute | solution.py:55
  194.9 17.9 %collective-permute-start.52 = (f32[8,128,128]{2,1,0:T(8,128)S(1)}, f32[8,128,128]{2,1,0:T(8,128)S(1)}, u32[]{:S(2)}, u32[]{:S(2)}) collective-permute-start(f32[8,128,128]{2,1,0:T(8,128)S(1)} %collective-permute-done.51.refs_47_), channel_id=1, source_target_pairs={{0,16},{1,17},{2,18},{3,19},{4,20},{5,21},{6,22},{7,23},{8,24},{9,... | collective-permute-start | bytes 1572872 | tf_op jit(solution)/shard_map/ppermute | solution.py:55
  (63 other events, 569.5 us)

commit v2 on v1

--- a/solution.py
+++ b/solution.py
@@ -51,8 +51,9 @@
 MOVE_C = _moves(lambda x, yl, z, yh, c: (x, yl, z, yh, 1 - c))
 
 
-def move(value, moves):
-    return lax.ppermute(value, AXES, moves)
+def move(value, moves, name):
+    with jax.named_scope(name):
+        return lax.ppermute(value, AXES, moves)
 
 
 def after(value, *others):
@@ -92,9 +93,9 @@
         + [pl.BlockSpec(memory_space=pltpu.HBM)] * n,
         out_specs=pl.BlockSpec(memory_space=pltpu.VMEM),
         scratch_shapes=[pltpu.SemaphoreType.DMA((2 * n,))],
-        compiler_params=pltpu.CompilerParams(vmem_limit_bytes=VMEM_LIMIT),
+        compiler_params=pltpu.CompilerParams(vmem_limit_bytes=SMALL_VMEM),
         name="pick_rows",
-    )(table, *pieces)
+    )(table, *in_hbm(pieces))
 
 
 def _start_left(table, left, lbuf, lsem, base, rows):
@@ -158,21 +159,36 @@
             ).wait()
 
 
-def _square_kernel(scale, n_rows, table, *refs):
-    left = refs[:SLOTS]
-    right = refs[SLOTS : SLOTS + 8]
-    out, lbuf, rpan, acc, lsem, rsem = refs[SLOTS + 8 :]
-    per = right[0].shape[0]
+def _stage_kernel(*refs):
+    pieces, panel, sems = refs[:-2], refs[-2], refs[-1]
+    per = pieces[0].shape[0]
     loads = [
-        pltpu.make_async_copy(right[q], rpan.at[pl.ds(q * per, per)], rsem.at[q])
-        for q in range(8)
+        pltpu.make_async_copy(piece, panel.at[pl.ds(q * per, per)], sems.at[q])
+        for q, piece in enumerate(pieces)
     ]
     for c in loads:
         c.start()
-    _start_left(table, left, lbuf, lsem, 0, n_rows)
-    rpan[ATOMS] = jnp.zeros((EDGE, EDGE), jnp.float32)
+    panel[ATOMS] = jnp.zeros((EDGE, EDGE), jnp.float32)
     for c in loads:
         c.wait()
+
+
+def stage_rows(pieces):
+    return pl.pallas_call(
+        _stage_kernel,
+        out_shape=pltpu.VMEM((ATOMS + 1, EDGE, EDGE), jnp.float32),
+        in_specs=[pl.BlockSpec(memory_space=pltpu.HBM)] * len(pieces),
+        out_specs=pl.BlockSpec(memory_space=pltpu.VMEM),
+        scratch_shapes=[pltpu.SemaphoreType.DMA((len(pieces),))],
+        compiler_params=pltpu.CompilerParams(vmem_limit_bytes=SMALL_VMEM),
+        name="stage_rows",
+    )(*in_hbm(pieces))
+
+
+def _square_kernel(scale, n_rows, table, *refs):
+    left = refs[:SLOTS]
+    rpan, out, lbuf, acc, lsem = refs[SLOTS:]
+    _start_left(table, left, lbuf, lsem, 0, n_rows)
 
     def row(t, carry):
         _wait_row(table, left, lbuf, lsem, t, t)
@@ -185,26 +201,31 @@
 
 MOST = 12
 VMEM_LIMIT = 58 * 2**20
-
-
-def square_rows(table, left, right, scale):
+SQUARE_VMEM = 44 * 2**20
+SMALL_VMEM = 4 * 2**20
+
+
+def in_hbm(values):
+    return [pltpu.with_memory_space_constraint(v, pltpu.HBM) for v in values]
+
+
+def square_rows(table, left, panel, scale):
     n_rows = left[0].shape[0]
     return pl.pallas_call(
         lambda *refs: _square_kernel(scale, n_rows, *refs),
         out_shape=jax.ShapeDtypeStruct((n_rows, EDGE, EDGE), jnp.float32),
         in_specs=[pl.BlockSpec(memory_space=pltpu.SMEM)]
-        + [pl.BlockSpec(memory_space=pltpu.HBM)] * (SLOTS + 8),
+        + [pl.BlockSpec(memory_space=pltpu.HBM)] * SLOTS
+        + [pl.BlockSpec(memory_space=pltpu.VMEM)],
         out_specs=pl.BlockSpec(memory_space=pltpu.VMEM),
         scratch_shapes=[
             pltpu.VMEM((n_rows, MOST, EDGE, EDGE), jnp.float32),
-            pltpu.VMEM((ATOMS + 1, EDGE, EDGE), jnp.float32),
             pltpu.VMEM((EDGE, EDGE), jnp.float32),
             pltpu.SemaphoreType.DMA((n_rows, SLOTS)),
-            pltpu.SemaphoreType.DMA((8,)),
         ],
-        compiler_params=pltpu.CompilerParams(vmem_limit_bytes=VMEM_LIMIT),
+        compiler_params=pltpu.CompilerParams(vmem_limit_bytes=SQUARE_VMEM),
         name="square_rows",
-    )(table, *left, *right)
+    )(table, *in_hbm(left), panel)
 
 
 def _update_kernel(scale, table, *refs):
@@ -281,7 +302,7 @@
         ],
         compiler_params=pltpu.CompilerParams(vmem_limit_bytes=VMEM_LIMIT),
         name="update_rows",
-    )(table, *left_a, *left_b, *right)
+    )(table, *in_hbm(left_a + left_b + right))
 
 
 def _mod4(v):
@@ -380,68 +401,68 @@
     scale = 1.0 / math.sqrt(12 * EDGE)
     blocks = atom_blocks[:, 0]
     pick_first, pick_rest, first_table, second_table = build_tables(grid_position, pattern)
-    a = move(blocks, MOVE_XA)
-    b = move(blocks, MOVE_XB)
-    w = move(blocks, MOVE_YP)
-    aa = move(a, MOVE_XA)
-    wa = move(w, MOVE_XA)
-    wb = move(w, MOVE_XB)
+    a = move(blocks, MOVE_XA, "a")
+    b = move(blocks, MOVE_XB, "b")
+    w = move(blocks, MOVE_YP, "w")
+    aa = move(a, MOVE_XA, "aa")
+    wa = move(w, MOVE_XA, "wa")
+    wb = move(w, MOVE_XB, "wb")
     rows_a = pick_rows([blocks, a, b, w], pick_first)
-    fa = move(rows_a, MOVE_ZA)
-    fb = move(rows_a, MOVE_ZB)
-    fy = move(rows_a, MOVE_YA)
-    fc = move(rows_a, MOVE_C)
-    fh = move(fy, MOVE_YA)
-    faa = move(after(fa, fy), MOVE_ZA)
-    waa = move(aa, MOVE_YP)
-    fca = move(after(fa, fb), MOVE_C)
-    fcb = move(fb, MOVE_C)
-    fha = move(after(fh, aa), MOVE_ZA)
-    fhb = move(after(fh, aa), MOVE_ZB)
-    fcaa = move(faa, MOVE_C)
-    fch = move(fh, MOVE_C)
+    fa = move(rows_a, MOVE_ZA, "fa")
+    fb = move(rows_a, MOVE_ZB, "fb")
+    fy = move(rows_a, MOVE_YA, "fy")
+    fc = move(rows_a, MOVE_C, "fc")
+    fh = move(fy, MOVE_YA, "fh")
+    faa = move(after(fa, fy), MOVE_ZA, "faa")
+    waa = move(aa, MOVE_YP, "waa")
+    fca = move(after(fa, fb), MOVE_C, "fca")
+    fcb = move(fb, MOVE_C, "fcb")
+    fha = move(after(fh, aa), MOVE_ZA, "fha")
+    fhb = move(after(fh, aa), MOVE_ZB, "fhb")
+    fcaa = move(faa, MOVE_C, "fcaa")
+    fch = move(fh, MOVE_C, "fch")
     rows_b = pick_rows([wa, wb, aa, waa], pick_rest)
-    sa = move(rows_b, MOVE_ZA)
-    sb = move(rows_b, MOVE_ZB)
-    sy = move(rows_b, MOVE_YA)
-    sc = move(rows_b, MOVE_C)
-    fhaa = move(after(fha, rows_b), MOVE_ZA)
-    fcha = move(after(fha, rows_b), MOVE_C)
-    fchb = move(fhb, MOVE_C)
-    fchaa = move(fhaa, MOVE_C)
+    sa = move(rows_b, MOVE_ZA, "sa")
+    sb = move(rows_b, MOVE_ZB, "sb")
+    sy = move(rows_b, MOVE_YA, "sy")
+    sc = move(rows_b, MOVE_C, "sc")
+    staged = stage_rows([blocks, a, b, w, wa, wb, aa, waa])
+    fhaa = move(after(fha, rows_b), MOVE_ZA, "fhaa")
+    fcha = move(after(fha, rows_b), MOVE_C, "fcha")
+    fchb = move(fhb, MOVE_C, "fchb")
+    fchaa = move(fhaa, MOVE_C, "fchaa")
     left_a = [rows_a, fa, fb, fh, fha, fhb, faa, fhaa]
     left_a += [fc, fca, fcb, fch, fcha, fchb, fcaa, fchaa]
-    right = [blocks, a, b, w, wa, wb, aa, waa]
-    square_a = square_rows(after(first_table[:HALF], sc), left_a, right, scale)
-    ga = move(square_a, MOVE_XA)
-    gb = move(square_a, MOVE_XB)
-    gw = move(square_a, MOVE_YP)
-    sh = move(after(sy, square_a), MOVE_YA)
-    saa = move(after(sa, square_a), MOVE_ZA)
-    sca = move(after(sa, square_a), MOVE_C)
-    scb = move(after(sb, square_a), MOVE_C)
-    gaa = move(after(ga, sy, sa), MOVE_XA)
-    gwa = move(after(gw, sy, sa, gb), MOVE_XA)
-    gwb = move(after(gw, sy, sa, gb), MOVE_XB)
-    sha = move(after(sh, gw, gb), MOVE_ZA)
-    shb = move(after(sh, gw, gb), MOVE_ZB)
-    sch = move(sh, MOVE_C)
-    scaa = move(saa, MOVE_C)
-    gwaa = move(after(gaa, sh), MOVE_YP)
-    shaa = move(after(sha, gaa), MOVE_ZA)
-    scha = move(after(sha, gaa), MOVE_C)
-    schb = move(shb, MOVE_C)
-    schaa = move(shaa, MOVE_C)
+    square_a = square_rows(after(first_table[:HALF], sc), left_a, staged, scale)
+    ga = move(square_a, MOVE_XA, "ga")
+    gb = move(square_a, MOVE_XB, "gb")
+    gw = move(square_a, MOVE_YP, "gw")
+    sh = move(after(sy, square_a), MOVE_YA, "sh")
+    saa = move(after(sa, square_a), MOVE_ZA, "saa")
+    sca = move(after(sa, square_a), MOVE_C, "sca")
+    scb = move(after(sb, square_a), MOVE_C, "scb")
+    gaa = move(after(ga, sy, sa), MOVE_XA, "gaa")
+    gwa = move(after(gw, sy, sa, gb), MOVE_XA, "gwa")
+    gwb = move(after(gw, sy, sa, gb), MOVE_XB, "gwb")
+    sha = move(after(sh, gw, gb), MOVE_ZA, "sha")
+    shb = move(after(sh, gw, gb), MOVE_ZB, "shb")
+    sch = move(sh, MOVE_C, "sch")
+    scaa = move(saa, MOVE_C, "scaa")
+    gwaa = move(after(gaa, sh), MOVE_YP, "gwaa")
+    shaa = move(after(sha, gaa), MOVE_ZA, "shaa")
+    scha = move(after(sha, gaa), MOVE_C, "scha")
+    schb = move(shb, MOVE_C, "schb")
+    schaa = move(shaa, MOVE_C, "schaa")
     left_b = [rows_b, sa, sb, sh, sha, shb, saa, shaa]
     left_b += [sc, sca, scb, sch, scha, schb, scaa, schaa]
-    square_b = square_rows(first_table[HALF:], left_b, right, scale)
-    ha = move(square_b, MOVE_XA)
-    hb = move(square_b, MOVE_XB)
-    hw = move(square_b, MOVE_YP)
-    haa = move(after(ha, gwa, gwb), MOVE_XA)
-    hwa = move(hw, MOVE_XA)
-    hwb = move(hw, MOVE_XB)
-    hwaa = move(haa, MOVE_YP)
+    square_b = square_rows(first_table[HALF:], left_b, staged, scale)
+    ha = move(square_b, MOVE_XA, "ha")
+    hb = move(square_b, MOVE_XB, "hb")
+    hw = move(square_b, MOVE_YP, "hw")
+    haa = move(after(ha, gwa, gwb), MOVE_XA, "haa")
+    hwa = move(hw, MOVE_XA, "hwa")
+    hwb = move(hw, MOVE_XB, "hwb")
+    hwaa = move(haa, MOVE_YP, "hwaa")
     panel = [square_a, ga, gb, gw, gwa, gwb, gaa, gwaa]
     panel += [square_b, ha, hb, hw, hwa, hwb, haa, hwaa]
     square, update = update_rows(second_table, left_a, left_b, panel, scale)

time: 230 us -> 224 us (0.974)
  starting transfers between devices: 66.2 us -> 59 us
  waiting for transfers between devices: 108 us -> 115 us
  Pallas kernels: 38 us -> 33.6 us
    ppermute x53, waiting for transfers between devices: 108 us -> 115 us  [move(): return lax.ppermute(value, AXES, moves)]
    ppermute x53, starting transfers between devices: 66.2 us -> 59 us  [move(): return lax.ppermute(value, AXES, moves)]
    pallas_call x2, Pallas kernels: 18.6 us -> 12.3 us  [square_rows(): pl.pallas_call(lambda *refs: _square_kernel(scale, n_rows, *refs), out_sh...]
    pallas_call x0 -> x1, Pallas kernels: none -> 3.47 us  [stage_rows(): pl.pallas_call(_stage_kernel, out_shape=pltpu.VMEM((ATOMS + 1, EDGE, EDGE...]
    unnamed x84 -> x90, local copies, waits for them, and re-layouts: 7.66 us -> 5.91 us
  transfers between devices with their start and end apart: 53 -> 53, of which waited for: 21 -> 18; matrix products, arithmetic and copies ran while one was open for 3% -> 4% of each run, Pallas kernels for 10% -> 9%
where the time goes in v2:
time: 224 us; the launch traced here: 223 us
  waiting for transfers between devices  115 us (51%)
  starting transfers between devices  59 us (26%)
  Pallas kernels  33.6 us (15%)
  local copies, waits for them, and re-layouts  7.13 us (3%)
  other arithmetic  6.8 us (3%)
    ppermute x53, waiting for transfers between devices, move(): return lax.ppermute(value, AXES, moves)  115 us
    ppermute x53, starting transfers between devices, move(): return lax.ppermute(value, AXES, moves)  59 us
    pallas_call x1, Pallas kernels, update_rows(): pl.pallas_call(lambda *refs: _update_kernel(scale, *refs), out_shape=(out...  14.4 us
    pallas_call x2, Pallas kernels, square_rows(): pl.pallas_call(lambda *refs: _square_kernel(scale, n_rows, *refs), out_sh...  12.3 us
    unnamed x90, local copies, waits for them, and re-layouts  5.91 us
  transfers between devices with their start and end apart: 53, of which 18 were waited for; matrix products, arithmetic and copies ran while one was open for 4% of the time, Pallas kernels for 9%

profile of v2, /device:TPU:1, one launch (start us, length us, event | category | flops | bytes accessed | tf_op | source)
XLA Modules:
  0.0 223.4 jit_solution(3172994227523502105)
XLA Ops:
  0.6 2.2 collective-permute-start.2
  6.7 22.6 %collective-permute-done.refs_1_ = f32[16,128,128]{2,1,0:T(8,128)} collective-permute-done((f32[16,128,128]{2,1,0:T(8,128)}, f32[16,128,128]{2,1,0:T(8,128)}, u32[]{:S(2)}, u32[]{:S(2)}) %collective-permute-start) | collective-permute-done | bytes 1048608 | tf_op jit(solution)/shard_map/a/ppermute | solution.py:56
  35.9 2.0 collective-permute-start.5
  37.9 3.8 %collective-permute-start.3 = (f32[8,128,128]{2,1,0:T(8,128)S(1)}, f32[8,128,128]{2,1,0:T(8,128)}, u32[]{:S(2)}, u32[]{:S(2)}) collective-permute-start(f32[8,128,128]{2,1,0:T(8,128)S(1)} %pick_rows.2.refs_1_), channel_id=1, source_target_pairs={{0,4},{1,13},{2,6},{3,15},{4,8},{5,1},{6,10},{7,3},{8,12},{9,5},{1... | collective-permute-start | bytes 1572872 | tf_op jit(solution)/shard_map/fa/ppermute | solution.py:56
  41.6 2.7 %collective-permute-start.11 = (f32[16,128,128]{2,1,0:T(8,128)}, f32[16,128,128]{2,1,0:T(8,128)S(1)}, u32[]{:S(2)}, u32[]{:S(2)}) collective-permute-start(f32[16,128,128]{2,1,0:T(8,128)} %copy-done.4), channel_id=1, source_target_pairs={{0,32},{1,97},{2,34},{3,99},{4,36},{5,101},{6,38},{7,103},{8,40},{... | collective-permute-start | bytes 3145736 | tf_op jit(solution)/shard_map/wa/ppermute | solution.py:56
  51.2 8.1 %collective-permute-done.6.refs_4_ = f32[8,128,128]{2,1,0:T(8,128)} collective-permute-done((f32[8,128,128]{2,1,0:T(8,128)}, f32[8,128,128]{2,1,0:T(8,128)}, u32[]{:S(2)}, u32[]{:S(2)}) %collective-permute-start.6) | collective-permute-done | bytes 524320 | tf_op jit(solution)/shard_map/fh/ppermute | solution.py:56
  59.3 3.2 %collective-permute-start.15 = (f32[8,128,128]{2,1,0:T(8,128)S(1)}, f32[8,128,128]{2,1,0:T(8,128)}, u32[]{:S(2)}, u32[]{:S(2)}) collective-permute-start(f32[8,128,128]{2,1,0:T(8,128)S(1)} %pick_rows.2.refs_1_), channel_id=1, source_target_pairs={{0,1},{1,0},{2,3},{3,2},{4,5},{5,4},{6,7},{7,6},{8,9},{9,8},{10,11... | collective-permute-start | bytes 1572872 | tf_op jit(solution)/shard_map/fc/ppermute | solution.py:56
  62.7 5.6 %collective-permute-done.12.refs_1_.refs_5_ = f32[16,128,128]{2,1,0:T(8,128)S(1)} collective-permute-done((f32[16,128,128]{2,1,0:T(8,128)}, f32[16,128,128]{2,1,0:T(8,128)S(1)}, u32[]{:S(2)}, u32[]{:S(2)}) %collective-permute-start.12) | collective-permute-done | bytes 1048608 | tf_op jit(solution)/shard_map/wb/ppermute | solution.py:56
  71.0 7.9 %collective-permute-done.13.refs_3_.refs_7_ = f32[16,128,128]{2,1,0:T(8,128)} collective-permute-done((f32[16,128,128]{2,1,0:T(8,128)}, f32[16,128,128]{2,1,0:T(8,128)}, u32[]{:S(2)}, u32[]{:S(2)}) %collective-permute-start.13) | collective-permute-done | bytes 1048608 | tf_op jit(solution)/shard_map/waa/ppermute | solution.py:56
  81.0 3.6 %collective-permute-start.18 = (f32[8,128,128]{2,1,0:T(8,128)}, f32[8,128,128]{2,1,0:T(8,128)S(1)}, u32[]{:S(2)}, u32[]{:S(2)}) collective-permute-start(f32[8,128,128]{2,1,0:T(8,128)} %collective-permute-done.6.refs_4_), channel_id=1, source_target_pairs={{0,1},{1,0},{2,3},{3,2},{4,5},{5,4},{6,7},{7,6},{8,9},{9,8},{10,11... | collective-permute-start | bytes 1572872 | tf_op jit(solution)/shard_map/fch/ppermute | solution.py:56
  86.3 5.8 %collective-permute-done.9.refs_6_ = f32[8,128,128]{2,1,0:T(8,128)S(1)} collective-permute-done((f32[8,128,128]{2,1,0:T(8,128)}, f32[8,128,128]{2,1,0:T(8,128)S(1)}, u32[]{:S(2)}, u32[]{:S(2)}) %collective-permute-start.9) | collective-permute-done | bytes 524320 | tf_op jit(solution)/shard_map/fhb/ppermute | solution.py:56
  92.1 5.1 %collective-permute-start.20 = (f32[8,128,128]{2,1,0:T(8,128)S(1)}, f32[8,128,128]{2,1,0:T(8,128)S(1)}, u32[]{:S(2)}, u32[]{:S(2)}) collective-permute-start(f32[8,128,128]{2,1,0:T(8,128)S(1)} %collective-permute-done.9.refs_6_), channel_id=1, source_target_pairs={{0,1},{1,0},{2,3},{3,2},{4,5},{5,4},{6,7},{7,6},{8,9},{9,8},{10,11... | collective-permute-start | bytes 1572872 | tf_op jit(solution)/shard_map/fchb/ppermute | solution.py:56
  99.3 3.5 %stage_rows.1.refs_17_ = f32[129,128,128]{2,1,0:T(8,128)S(1)} custom-call(f32[16,128,128]{2,1,0:T(8,128)} %bitcast.17, f32[16,128,128]{2,1,0:T(8,128)} %collective-permute-done.refs_1_, f32[16,128,128]{2,1,0:T(8,128)} %copy-done.5, f32[16,128,128]{2,1,0:T(8,128)} %copy-done.4, f32[16,128,128]{2,1,0:T(8,128)} %copy-done.7, f32[16,128,128]{2,1,0:T(8,128)} %copy-done.6, ...), custom_call_target="tpu_custom_call" | custom-call | tf_op jit(solution)/shard_map/stage_rows/pallas_call | solution.py:177
  102.9 3.0 %collective-permute-start.23 = (f32[8,128,128]{2,1,0:T(8,128)S(1)}, f32[8,128,128]{2,1,0:T(8,128)S(1)}, u32[]{:S(2)}, u32[]{:S(2)}) collective-permute-start(f32[8,128,128]{2,1,0:T(8,128)S(1)} %pick_rows.3.refs_1_.refs_17_), channel_id=1, source_target_pairs={{0,4},{1,13},{2,6},{3,15},{4,8},{5,1},{6,10},{7,3},{8,12},{9,5},{1... | collective-permute-start | bytes 1572872 | tf_op jit(solution)/shard_map/sa/ppermute | solution.py:56
  107.7 6.2 %square_rows.2.refs_33_ = f32[8,128,128]{2,1,0:T(8,128)S(1)} custom-call(s32[8,64]{1,0:T(8,128)S(1)} %get-tuple-element.22.refs_0_, f32[8,128,128]{2,1,0:T(8,128)} %copy-done, f32[8,128,128]{2,1,0:T(8,128)} %collective-permute-done.3.refs_2_, f32[8,128,128]{2,1,0:T(8,128)} %collective-permute-done.4.refs_3_, f32[8,128,128]{2,1,0:T(8,128)} %collective-permute-done.6.refs_4_, ...), custom_call_target="tpu_custom_call" | custom-call | tf_op jit(solution)/shard_map/square_rows/pallas_call | solution.py:214
  113.9 3.0 %collective-permute-start.33 = (f32[8,128,128]{2,1,0:T(8,128)S(1)}, f32[8,128,128]{2,1,0:T(8,128)S(1)}, u32[]{:S(2)}, u32[]{:S(2)}) collective-permute-start(f32[8,128,128]{2,1,0:T(8,128)S(1)} %square_rows.2.refs_33_), channel_id=1, source_target_pairs={{0,32},{1,97},{2,34},{3,99},{4,36},{5,101},{6,38},{7,103},{8,40},{... | collective-permute-start | bytes 1572872 | tf_op jit(solution)/shard_map/ga/ppermute | solution.py:56
  118.5 9.3 %collective-permute-done.33.refs_34_ = f32[8,128,128]{2,1,0:T(8,128)S(1)} collective-permute-done((f32[8,128,128]{2,1,0:T(8,128)S(1)}, f32[8,128,128]{2,1,0:T(8,128)S(1)}, u32[]{:S(2)}, u32[]{:S(2)}) %collective-permute-start.33) | collective-permute-done | bytes 524320 | tf_op jit(solution)/shard_map/ga/ppermute | solution.py:56
  127.8 2.4 %collective-permute-start.34 = (f32[8,128,128]{2,1,0:T(8,128)S(1)}, f32[8,128,128]{2,1,0:T(8,128)S(1)}, u32[]{:S(2)}, u32[]{:S(2)}) collective-permute-start(f32[8,128,128]{2,1,0:T(8,128)S(1)} %collective-permute-done.33.refs_34_), channel_id=1, source_target_pairs={{0,32},{1,97},{2,34},{3,99},{4,36},{5,101},{6,38},{7,103},{8,40},{... | collective-permute-start | bytes 1572872 | tf_op jit(solution)/shard_map/gaa/ppermute | solution.py:56
  130.3 4.7 %collective-permute-done.28.refs_36_ = f32[8,128,128]{2,1,0:T(8,128)S(1)} collective-permute-done((f32[8,128,128]{2,1,0:T(8,128)S(1)}, f32[8,128,128]{2,1,0:T(8,128)S(1)}, u32[]{:S(2)}, u32[]{:S(2)}) %collective-permute-start.28) | collective-permute-done | bytes 524320 | tf_op jit(solution)/shard_map/gw/ppermute | solution.py:56
  137.3 8.7 %collective-permute-done.30.refs_5_.refs_21_ = f32[8,128,128]{2,1,0:T(8,128)S(1)} collective-permute-done((f32[8,128,128]{2,1,0:T(8,128)S(1)}, f32[8,128,128]{2,1,0:T(8,128)S(1)}, u32[]{:S(2)}, u32[]{:S(2)}) %collective-permute-start.30) | collective-permute-done | bytes 524320 | tf_op jit(solution)/shard_map/sha/ppermute | solution.py:56
  146.4 8.1 %collective-permute-done.32.refs_7_.refs_23_ = f32[8,128,128]{2,1,0:T(8,128)S(1)} collective-permute-done((f32[8,128,128]{2,1,0:T(8,128)S(1)}, f32[8,128,128]{2,1,0:T(8,128)S(1)}, u32[]{:S(2)}, u32[]{:S(2)}) %collective-permute-start.32) | collective-permute-done | bytes 524320 | tf_op jit(solution)/shard_map/saa/ppermute | solution.py:56
  155.1 4.7 %collective-permute-done.35.refs_8_.refs_24_ = f32[8,128,128]{2,1,0:T(8,128)S(1)} collective-permute-done((f32[8,128,128]{2,1,0:T(8,128)S(1)}, f32[8,128,128]{2,1,0:T(8,128)S(1)}, u32[]{:S(2)}, u32[]{:S(2)}) %collective-permute-start.35) | collective-permute-done | bytes 524320 | tf_op jit(solution)/shard_map/shaa/ppermute | solution.py:56
  159.9 2.6 %collective-permute-start.43 = (f32[8,128,128]{2,1,0:T(8,128)S(1)}, f32[8,128,128]{2,1,0:T(8,128)S(1)}, u32[]{:S(2)}, u32[]{:S(2)}) collective-permute-start(f32[8,128,128]{2,1,0:T(8,128)S(1)} %collective-permute-done.28.refs_36_), channel_id=1, source_target_pairs={{0,32},{1,97},{2,34},{3,99},{4,36},{5,101},{6,38},{7,103},{8,40},{... | collective-permute-start | bytes 1572872 | tf_op jit(solution)/shard_map/gwa/ppermute | solution.py:56
  163.7 6.1 %square_rows.3.refs_41_ = f32[8,128,128]{2,1,0:T(8,128)S(1)} custom-call(s32[8,64]{1,0:T(8,128)S(1)} %get-tuple-element.58.refs_0_, f32[8,128,128]{2,1,0:T(8,128)} %copy-done.1, f32[8,128,128]{2,1,0:T(8,128)} %copy-done.17, f32[8,128,128]{2,1,0:T(8,128)} %copy-done.19, f32[8,128,128]{2,1,0:T(8,128)} %copy-done.18, f32[8,128,128]{2,1,0:T(8,128)} %copy-done.20, ...), custom_call_target="tpu_custom_call" | custom-call | tf_op jit(solution)/shard_map/square_rows/pallas_call | solution.py:214
  171.4 1.9 collective-permute-done.44.refs_38_
  173.4 6.2 %collective-permute-done.46.refs_42_ = f32[8,128,128]{2,1,0:T(8,128)S(1)} collective-permute-done((f32[8,128,128]{2,1,0:T(8,128)S(1)}, f32[8,128,128]{2,1,0:T(8,128)S(1)}, u32[]{:S(2)}, u32[]{:S(2)}) %collective-permute-start.46) | collective-permute-done | bytes 524320 | tf_op jit(solution)/shard_map/ha/ppermute | solution.py:56
  179.6 2.1 collective-permute-start.51
  186.0 4.3 %collective-permute-done.51.refs_47_ = f32[8,128,128]{2,1,0:T(8,128)S(1)} collective-permute-done((f32[8,128,128]{2,1,0:T(8,128)S(1)}, f32[8,128,128]{2,1,0:T(8,128)S(1)}, u32[]{:S(2)}, u32[]{:S(2)}) %collective-permute-start.51) | collective-permute-done | bytes 524320 | tf_op jit(solution)/shard_map/haa/ppermute | solution.py:56
  191.9 3.6 %collective-permute-done.45.refs_40_ = f32[8,128,128]{2,1,0:T(8,128)S(1)} collective-permute-done((f32[8,128,128]{2,1,0:T(8,128)S(1)}, f32[8,128,128]{2,1,0:T(8,128)S(1)}, u32[]{:S(2)}, u32[]{:S(2)}) %collective-permute-start.45) | collective-permute-done | bytes 524320 | tf_op jit(solution)/shard_map/gwaa/ppermute | solution.py:56
  195.5 3.0 %collective-permute-done.47.refs_43_ = f32[8,128,128]{2,1,0:T(8,128)S(1)} collective-permute-done((f32[8,128,128]{2,1,0:T(8,128)S(1)}, f32[8,128,128]{2,1,0:T(8,128)S(1)}, u32[]{:S(2)}, u32[]{:S(2)}) %collective-permute-start.47) | collective-permute-done | bytes 524320 | tf_op jit(solution)/shard_map/hb/ppermute | solution.py:56
  198.5 9.2 %collective-permute-done.50.refs_46_ = f32[8,128,128]{2,1,0:T(8,128)S(1)} collective-permute-done((f32[8,128,128]{2,1,0:T(8,128)S(1)}, f32[8,128,128]{2,1,0:T(8,128)S(1)}, u32[]{:S(2)}, u32[]{:S(2)}) %collective-permute-start.50) | collective-permute-done | bytes 524320 | tf_op jit(solution)/shard_map/hwb/ppermute | solution.py:56
  208.8 14.4 %update_rows.1 = (f32[16,128,128]{2,1,0:T(8,128)}, f32[16,128,128]{2,1,0:T(8,128)}) custom-call(s32[16,64]{1,0:T(8,128)} %get-tuple-element.57.refs_0_, f32[8,128,128]{2,1,0:T(8,128)} %copy-done, f32[8,128,128]{2,1,0:T(8,128)} %collective-permute-done.3.refs_2_, f32[8,128,128]{2,1,0:T(8,128)} %collective-permute-done.4.refs_3_, ...), custom_call_target="tpu_custom_call" | custom-call | tf_op jit(solution)/shard_map/update_rows/pallas_call | solution.py:288
  (208 shorter events, 42.4 us)
Async XLA Ops:
  0.6 31.6 %collective-permute-start.2 = (f32[16,128,128]{2,1,0:T(8,128)}, f32[16,128,128]{2,1,0:T(8,128)S(1)}, u32[]{:S(2)}, u32[]{:S(2)}) collective-permute-start(f32[16,128,128]{2,1,0:T(8,128)} %bitcast.13), channel_id=1, source_target_pairs={{0,16},{1,17},{2,18},{3,19},{4,20},{5,21},{6,22},{7,23},{8,24},{9,... | collective-permute-start | bytes 3145736 | tf_op jit(solution)/shard_map/w/ppermute | solution.py:56
  2.8 29.5 %collective-permute-start.1 = (f32[16,128,128]{2,1,0:T(8,128)}, f32[16,128,128]{2,1,0:T(8,128)S(1)}, u32[]{:S(2)}, u32[]{:S(2)}) collective-permute-start(f32[16,128,128]{2,1,0:T(8,128)} %bitcast.14), channel_id=1, source_target_pairs={{0,96},{1,33},{2,98},{3,35},{4,100},{5,37},{6,102},{7,39},{8,104},... | collective-permute-start | bytes 3145736 | tf_op jit(solution)/shard_map/b/ppermute | solution.py:56
  4.0 25.3 %collective-permute-start = (f32[16,128,128]{2,1,0:T(8,128)}, f32[16,128,128]{2,1,0:T(8,128)}, u32[]{:S(2)}, u32[]{:S(2)}) collective-permute-start(f32[16,128,128]{2,1,0:T(8,128)} %bitcast.15), channel_id=1, source_target_pairs={{0,32},{1,97},{2,34},{3,99},{4,36},{5,101},{6,38},{7,103},{8,40},{... | collective-permute-start | bytes 3145736 | tf_op jit(solution)/shard_map/a/ppermute | solution.py:56
  29.3 19.8 %collective-permute-start.7 = (f32[16,128,128]{2,1,0:T(8,128)}, f32[16,128,128]{2,1,0:T(8,128)}, u32[]{:S(2)}, u32[]{:S(2)}) collective-permute-start(f32[16,128,128]{2,1,0:T(8,128)} %collective-permute-done.refs_1_), channel_id=1, source_target_pairs={{0,32},{1,97},{2,34},{3,99},{4,36},{5,101},{6,38},{7,103},{8,40},{... | collective-permute-start | bytes 3145736 | tf_op jit(solution)/shard_map/aa/ppermute | solution.py:56
  41.6 26.7 %collective-permute-start.12 = (f32[16,128,128]{2,1,0:T(8,128)}, f32[16,128,128]{2,1,0:T(8,128)S(1)}, u32[]{:S(2)}, u32[]{:S(2)}) collective-permute-start(f32[16,128,128]{2,1,0:T(8,128)} %copy-done.4), channel_id=1, source_target_pairs={{0,96},{1,33},{2,98},{3,35},{4,100},{5,37},{6,102},{7,39},{8,104},... | collective-permute-start | bytes 3145736 | tf_op jit(solution)/shard_map/wb/ppermute | solution.py:56
  41.6 26.7 %collective-permute-start.11 = (f32[16,128,128]{2,1,0:T(8,128)}, f32[16,128,128]{2,1,0:T(8,128)S(1)}, u32[]{:S(2)}, u32[]{:S(2)}) collective-permute-start(f32[16,128,128]{2,1,0:T(8,128)} %copy-done.4), channel_id=1, source_target_pairs={{0,32},{1,97},{2,34},{3,99},{4,36},{5,101},{6,38},{7,103},{8,40},{... | collective-permute-start | bytes 3145736 | tf_op jit(solution)/shard_map/wa/ppermute | solution.py:56
  44.9 17.5 %collective-permute-start.4 = (f32[8,128,128]{2,1,0:T(8,128)S(1)}, f32[8,128,128]{2,1,0:T(8,128)}, u32[]{:S(2)}, u32[]{:S(2)}) collective-permute-start(f32[8,128,128]{2,1,0:T(8,128)S(1)} %pick_rows.2.refs_1_), channel_id=1, source_target_pairs={{0,12},{1,5},{2,14},{3,7},{4,0},{5,9},{6,2},{7,11},{8,4},{9,13},{1... | collective-permute-start | bytes 1572872 | tf_op jit(solution)/shard_map/fb/ppermute | solution.py:56
  49.2 29.7 %collective-permute-start.13 = (f32[16,128,128]{2,1,0:T(8,128)}, f32[16,128,128]{2,1,0:T(8,128)}, u32[]{:S(2)}, u32[]{:S(2)}) collective-permute-start(f32[16,128,128]{2,1,0:T(8,128)} %collective-permute-done.7.refs_2_.refs_6_), channel_id=1, source_target_pairs={{0,16},{1,17},{2,18},{3,19},{4,20},{5,21},{6,22},{7,23},{8,24},{9,... | collective-permute-start | bytes 3145736 | tf_op jit(solution)/shard_map/waa/ppermute | solution.py:56
  59.3 21.7 %collective-permute-start.15 = (f32[8,128,128]{2,1,0:T(8,128)S(1)}, f32[8,128,128]{2,1,0:T(8,128)}, u32[]{:S(2)}, u32[]{:S(2)}) collective-permute-start(f32[8,128,128]{2,1,0:T(8,128)S(1)} %pick_rows.2.refs_1_), channel_id=1, source_target_pairs={{0,1},{1,0},{2,3},{3,2},{4,5},{5,4},{6,7},{7,6},{8,9},{9,8},{10,11... | collective-permute-start | bytes 1572872 | tf_op jit(solution)/shard_map/fc/ppermute | solution.py:56
  62.5 22.3 %collective-permute-start.10 = (f32[8,128,128]{2,1,0:T(8,128)}, f32[8,128,128]{2,1,0:T(8,128)}, u32[]{:S(2)}, u32[]{:S(2)}) collective-permute-start(f32[8,128,128]{2,1,0:T(8,128)} %collective-permute-done.3.refs_2_), channel_id=1, source_target_pairs={{0,4},{1,13},{2,6},{3,15},{4,8},{5,1},{6,10},{7,3},{8,12},{9,5},{1... | collective-permute-start | bytes 1572872 | tf_op jit(solution)/shard_map/faa/ppermute | solution.py:56
  68.3 16.3 %collective-permute-start.17 = (f32[8,128,128]{2,1,0:T(8,128)}, f32[8,128,128]{2,1,0:T(8,128)}, u32[]{:S(2)}, u32[]{:S(2)}) collective-permute-start(f32[8,128,128]{2,1,0:T(8,128)} %collective-permute-done.4.refs_3_), channel_id=1, source_target_pairs={{0,1},{1,0},{2,3},{3,2},{4,5},{5,4},{6,7},{7,6},{8,9},{9,8},{10,11... | collective-permute-start | bytes 1572872 | tf_op jit(solution)/shard_map/fcb/ppermute | solution.py:56
  81.0 16.2 %collective-permute-start.18 = (f32[8,128,128]{2,1,0:T(8,128)}, f32[8,128,128]{2,1,0:T(8,128)S(1)}, u32[]{:S(2)}, u32[]{:S(2)}) collective-permute-start(f32[8,128,128]{2,1,0:T(8,128)} %collective-permute-done.6.refs_4_), channel_id=1, source_target_pairs={{0,1},{1,0},{2,3},{3,2},{4,5},{5,4},{6,7},{7,6},{8,9},{9,8},{10,11... | collective-permute-start | bytes 1572872 | tf_op jit(solution)/shard_map/fch/ppermute | solution.py:56
  85.8 17.1 %collective-permute-start.21 = (f32[8,128,128]{2,1,0:T(8,128)}, f32[8,128,128]{2,1,0:T(8,128)S(1)}, u32[]{:S(2)}, u32[]{:S(2)}) collective-permute-start(f32[8,128,128]{2,1,0:T(8,128)} %collective-permute-done.10.refs_7_), channel_id=1, source_target_pairs={{0,1},{1,0},{2,3},{3,2},{4,5},{5,4},{6,7},{7,6},{8,9},{9,8},{10,11... | collective-permute-start | bytes 1572872 | tf_op jit(solution)/shard_map/fcaa/ppermute | solution.py:56
  92.1 13.8 %collective-permute-start.20 = (f32[8,128,128]{2,1,0:T(8,128)S(1)}, f32[8,128,128]{2,1,0:T(8,128)S(1)}, u32[]{:S(2)}, u32[]{:S(2)}) collective-permute-start(f32[8,128,128]{2,1,0:T(8,128)S(1)} %collective-permute-done.9.refs_6_), channel_id=1, source_target_pairs={{0,1},{1,0},{2,3},{3,2},{4,5},{5,4},{6,7},{7,6},{8,9},{9,8},{10,11... | collective-permute-start | bytes 1572872 | tf_op jit(solution)/shard_map/fchb/ppermute | solution.py:56
  97.3 19.6 %collective-permute-start.25 = (f32[8,128,128]{2,1,0:T(8,128)S(1)}, f32[8,128,128]{2,1,0:T(8,128)S(1)}, u32[]{:S(2)}, u32[]{:S(2)}) collective-permute-start(f32[8,128,128]{2,1,0:T(8,128)S(1)} %pick_rows.3.refs_1_.refs_17_), channel_id=1, source_target_pairs={{0,16},{1,19},{2,18},{3,17},{4,20},{5,23},{6,22},{7,21},{8,24},{9,... | collective-permute-start | bytes 1572872 | tf_op jit(solution)/shard_map/sy/ppermute | solution.py:56
  102.9 15.6 %collective-permute-start.23 = (f32[8,128,128]{2,1,0:T(8,128)S(1)}, f32[8,128,128]{2,1,0:T(8,128)S(1)}, u32[]{:S(2)}, u32[]{:S(2)}) collective-permute-start(f32[8,128,128]{2,1,0:T(8,128)S(1)} %pick_rows.3.refs_1_.refs_17_), channel_id=1, source_target_pairs={{0,4},{1,13},{2,6},{3,15},{4,8},{5,1},{6,10},{7,3},{8,12},{9,5},{1... | collective-permute-start | bytes 1572872 | tf_op jit(solution)/shard_map/sa/ppermute | solution.py:56
  113.9 13.8 %collective-permute-start.33 = (f32[8,128,128]{2,1,0:T(8,128)S(1)}, f32[8,128,128]{2,1,0:T(8,128)S(1)}, u32[]{:S(2)}, u32[]{:S(2)}) collective-permute-start(f32[8,128,128]{2,1,0:T(8,128)S(1)} %square_rows.2.refs_33_), channel_id=1, source_target_pairs={{0,32},{1,97},{2,34},{3,99},{4,36},{5,101},{6,38},{7,103},{8,40},{... | collective-permute-start | bytes 1572872 | tf_op jit(solution)/shard_map/ga/ppermute | solution.py:56
  117.8 17.1 %collective-permute-start.28 = (f32[8,128,128]{2,1,0:T(8,128)S(1)}, f32[8,128,128]{2,1,0:T(8,128)S(1)}, u32[]{:S(2)}, u32[]{:S(2)}) collective-permute-start(f32[8,128,128]{2,1,0:T(8,128)S(1)} %square_rows.2.refs_33_), channel_id=1, source_target_pairs={{0,16},{1,17},{2,18},{3,19},{4,20},{5,21},{6,22},{7,23},{8,24},{9,... | collective-permute-start | bytes 1572872 | tf_op jit(solution)/shard_map/gw/ppermute | solution.py:56
  118.4 17.0 %collective-permute-start.24 = (f32[8,128,128]{2,1,0:T(8,128)S(1)}, f32[8,128,128]{2,1,0:T(8,128)S(1)}, u32[]{:S(2)}, u32[]{:S(2)}) collective-permute-start(f32[8,128,128]{2,1,0:T(8,128)S(1)} %pick_rows.3.refs_1_.refs_17_), channel_id=1, source_target_pairs={{0,12},{1,5},{2,14},{3,7},{4,0},{5,9},{6,2},{7,11},{8,4},{9,13},{1... | collective-permute-start | bytes 1572872 | tf_op jit(solution)/shard_map/sb/ppermute | solution.py:56
  135.3 19.1 %collective-permute-start.32 = (f32[8,128,128]{2,1,0:T(8,128)S(1)}, f32[8,128,128]{2,1,0:T(8,128)S(1)}, u32[]{:S(2)}, u32[]{:S(2)}) collective-permute-start(f32[8,128,128]{2,1,0:T(8,128)S(1)} %collective-permute-done.23.refs_2_.refs_18_), channel_id=1, source_target_pairs={{0,4},{1,13},{2,6},{3,15},{4,8},{5,1},{6,10},{7,3},{8,12},{9,5},{1... | collective-permute-start | bytes 1572872 | tf_op jit(solution)/shard_map/saa/ppermute | solution.py:56
  135.4 19.1 %collective-permute-start.37 = (f32[8,128,128]{2,1,0:T(8,128)S(1)}, f32[8,128,128]{2,1,0:T(8,128)S(1)}, u32[]{:S(2)}, u32[]{:S(2)}) collective-permute-start(f32[8,128,128]{2,1,0:T(8,128)S(1)} %collective-permute-done.24.refs_3_.refs_19_), channel_id=1, source_target_pairs={{0,1},{1,0},{2,3},{3,2},{4,5},{5,4},{6,7},{7,6},{8,9},{9,8},{10,11... | collective-permute-start | bytes 1572872 | tf_op jit(solution)/shard_map/scb/ppermute | solution.py:56
  137.2 17.8 %collective-permute-start.31 = (f32[8,128,128]{2,1,0:T(8,128)S(1)}, f32[8,128,128]{2,1,0:T(8,128)S(1)}, u32[]{:S(2)}, u32[]{:S(2)}) collective-permute-start(f32[8,128,128]{2,1,0:T(8,128)S(1)} %collective-permute-done.27.refs_4_.refs_20_), channel_id=1, source_target_pairs={{0,12},{1,5},{2,14},{3,7},{4,0},{5,9},{6,2},{7,11},{8,4},{9,13},{1... | collective-permute-start | bytes 1572872 | tf_op jit(solution)/shard_map/shb/ppermute | solution.py:56
  146.0 13.8 %collective-permute-start.35 = (f32[8,128,128]{2,1,0:T(8,128)S(1)}, f32[8,128,128]{2,1,0:T(8,128)S(1)}, u32[]{:S(2)}, u32[]{:S(2)}) collective-permute-start(f32[8,128,128]{2,1,0:T(8,128)S(1)} %collective-permute-done.30.refs_5_.refs_21_), channel_id=1, source_target_pairs={{0,4},{1,13},{2,6},{3,15},{4,8},{5,1},{6,10},{7,3},{8,12},{9,5},{1... | collective-permute-start | bytes 1572872 | tf_op jit(solution)/shard_map/shaa/ppermute | solution.py:56
  146.4 13.4 %collective-permute-start.38 = (f32[8,128,128]{2,1,0:T(8,128)S(1)}, f32[8,128,128]{2,1,0:T(8,128)S(1)}, u32[]{:S(2)}, u32[]{:S(2)}) collective-permute-start(f32[8,128,128]{2,1,0:T(8,128)S(1)} %collective-permute-done.27.refs_4_.refs_20_), channel_id=1, source_target_pairs={{0,1},{1,0},{2,3},{3,2},{4,5},{5,4},{6,7},{7,6},{8,9},{9,8},{10,11... | collective-permute-start | bytes 1572872 | tf_op jit(solution)/shard_map/sch/ppermute | solution.py:56
  159.8 13.5 %collective-permute-start.44 = (f32[8,128,128]{2,1,0:T(8,128)S(1)}, f32[8,128,128]{2,1,0:T(8,128)S(1)}, u32[]{:S(2)}, u32[]{:S(2)}) collective-permute-start(f32[8,128,128]{2,1,0:T(8,128)S(1)} %collective-permute-done.28.refs_36_), channel_id=1, source_target_pairs={{0,96},{1,33},{2,98},{3,35},{4,100},{5,37},{6,102},{7,39},{8,104},... | collective-permute-start | bytes 1572872 | tf_op jit(solution)/shard_map/gwb/ppermute | solution.py:56
  159.9 13.4 %collective-permute-start.43 = (f32[8,128,128]{2,1,0:T(8,128)S(1)}, f32[8,128,128]{2,1,0:T(8,128)S(1)}, u32[]{:S(2)}, u32[]{:S(2)}) collective-permute-start(f32[8,128,128]{2,1,0:T(8,128)S(1)} %collective-permute-done.28.refs_36_), channel_id=1, source_target_pairs={{0,32},{1,97},{2,34},{3,99},{4,36},{5,101},{6,38},{7,103},{8,40},{... | collective-permute-start | bytes 1572872 | tf_op jit(solution)/shard_map/gwa/ppermute | solution.py:56
  169.9 13.5 %collective-permute-start.48 = (f32[8,128,128]{2,1,0:T(8,128)S(1)}, f32[8,128,128]{2,1,0:T(8,128)S(1)}, u32[]{:S(2)}, u32[]{:S(2)}) collective-permute-start(f32[8,128,128]{2,1,0:T(8,128)S(1)} %square_rows.3.refs_41_), channel_id=1, source_target_pairs={{0,16},{1,17},{2,18},{3,19},{4,20},{5,21},{6,22},{7,23},{8,24},{9,... | collective-permute-start | bytes 1572872 | tf_op jit(solution)/shard_map/hw/ppermute | solution.py:56
  181.7 13.8 %collective-permute-start.45 = (f32[8,128,128]{2,1,0:T(8,128)S(1)}, f32[8,128,128]{2,1,0:T(8,128)S(1)}, u32[]{:S(2)}, u32[]{:S(2)}) collective-permute-start(f32[8,128,128]{2,1,0:T(8,128)S(1)} %collective-permute-done.34.refs_39_), channel_id=1, source_target_pairs={{0,16},{1,17},{2,18},{3,19},{4,20},{5,21},{6,22},{7,23},{8,24},{9,... | collective-permute-start | bytes 1572872 | tf_op jit(solution)/shard_map/gwaa/ppermute | solution.py:56
  183.2 15.2 %collective-permute-start.47 = (f32[8,128,128]{2,1,0:T(8,128)S(1)}, f32[8,128,128]{2,1,0:T(8,128)S(1)}, u32[]{:S(2)}, u32[]{:S(2)}) collective-permute-start(f32[8,128,128]{2,1,0:T(8,128)S(1)} %square_rows.3.refs_41_), channel_id=1, source_target_pairs={{0,96},{1,33},{2,98},{3,35},{4,100},{5,37},{6,102},{7,39},{8,104},... | collective-permute-start | bytes 1572872 | tf_op jit(solution)/shard_map/hb/ppermute | solution.py:56
  183.4 24.3 %collective-permute-start.50 = (f32[8,128,128]{2,1,0:T(8,128)S(1)}, f32[8,128,128]{2,1,0:T(8,128)S(1)}, u32[]{:S(2)}, u32[]{:S(2)}) collective-permute-start(f32[8,128,128]{2,1,0:T(8,128)S(1)} %collective-permute-done.48.refs_44_), channel_id=1, source_target_pairs={{0,96},{1,33},{2,98},{3,35},{4,100},{5,37},{6,102},{7,39},{8,104},... | collective-permute-start | bytes 1572872 | tf_op jit(solution)/shard_map/hwb/ppermute | solution.py:56
  184.6 23.0 %collective-permute-start.49 = (f32[8,128,128]{2,1,0:T(8,128)S(1)}, f32[8,128,128]{2,1,0:T(8,128)S(1)}, u32[]{:S(2)}, u32[]{:S(2)}) collective-permute-start(f32[8,128,128]{2,1,0:T(8,128)S(1)} %collective-permute-done.48.refs_44_), channel_id=1, source_target_pairs={{0,32},{1,97},{2,34},{3,99},{4,36},{5,101},{6,38},{7,103},{8,40},{... | collective-permute-start | bytes 1572872 | tf_op jit(solution)/shard_map/hwa/ppermute | solution.py:56
  190.3 17.3 %collective-permute-start.52 = (f32[8,128,128]{2,1,0:T(8,128)S(1)}, f32[8,128,128]{2,1,0:T(8,128)S(1)}, u32[]{:S(2)}, u32[]{:S(2)}) collective-permute-start(f32[8,128,128]{2,1,0:T(8,128)S(1)} %collective-permute-done.51.refs_47_), channel_id=1, source_target_pairs={{0,16},{1,17},{2,18},{3,19},{4,20},{5,21},{6,22},{7,23},{8,24},{9,... | collective-permute-start | bytes 1572872 | tf_op jit(solution)/shard_map/hwaa/ppermute | solution.py:56
  (66 other events, 962.5 us)

commit v3 on v2

--- a/solution.py
+++ b/solution.py
@@ -95,7 +95,7 @@
         scratch_shapes=[pltpu.SemaphoreType.DMA((2 * n,))],
         compiler_params=pltpu.CompilerParams(vmem_limit_bytes=SMALL_VMEM),
         name="pick_rows",
-    )(table, *in_hbm(pieces))
+    )(table, *pieces)
 
 
 def _start_left(table, left, lbuf, lsem, base, rows):
@@ -231,17 +231,16 @@
 def _update_kernel(scale, table, *refs):
     left_a = refs[:SLOTS]
     left_b = refs[SLOTS : 2 * SLOTS]
-    right = refs[2 * SLOTS : 2 * SLOTS + 16]
-    square, update, lbuf, rpan, acc, ubuf, lsem, rsem, ssem, usem = refs[2 * SLOTS + 16 :]
+    right = refs[2 * SLOTS + 1 : 2 * SLOTS + 9]
+    square, update, rpan, lbuf, acc, ubuf, lsem, rsem, ssem, usem = refs[2 * SLOTS + 9 :]
     loads = [
-        pltpu.make_async_copy(right[q], rpan.at[pl.ds(q * HALF, HALF)], rsem.at[q])
-        for q in range(16)
+        pltpu.make_async_copy(right[q], rpan.at[pl.ds(64 + q * HALF, HALF)], rsem.at[q])
+        for q in range(8)
     ]
     for c in loads:
         c.start()
     _start_left(table, left_a, lbuf, lsem, 0, HALF)
     _start_left(table, left_b, lbuf, lsem, HALF, HALF)
-    rpan[ATOMS] = jnp.zeros((EDGE, EDGE), jnp.float32)
     for c in loads:
         c.wait()
     squares = [
@@ -282,17 +281,18 @@
         c.wait()
 
 
-def update_rows(table, left_a, left_b, right, scale):
+def update_rows(table, left_a, left_b, staged, right, scale):
     out = jax.ShapeDtypeStruct((ROWS, EDGE, EDGE), jnp.float32)
     hbm = pl.BlockSpec(memory_space=pltpu.HBM)
+    vmem = pl.BlockSpec(memory_space=pltpu.VMEM)
     return pl.pallas_call(
         lambda *refs: _update_kernel(scale, *refs),
-        out_shape=(out, out),
-        in_specs=[pl.BlockSpec(memory_space=pltpu.SMEM)] + [hbm] * (2 * SLOTS + 16),
-        out_specs=(hbm, hbm),
+        out_shape=(out, out, pltpu.VMEM((ATOMS + 1, EDGE, EDGE), jnp.float32)),
+        input_output_aliases={1 + 2 * SLOTS: 2},
+        in_specs=[pl.BlockSpec(memory_space=pltpu.SMEM)] + [hbm] * (2 * SLOTS) + [vmem] + [hbm] * 8,
+        out_specs=(hbm, hbm, vmem),
         scratch_shapes=[
             pltpu.VMEM((ROWS, MOST, EDGE, EDGE), jnp.float32),
-            pltpu.VMEM((ATOMS + 1, EDGE, EDGE), jnp.float32),
             pltpu.VMEM((EDGE, EDGE), jnp.float32),
             pltpu.VMEM((ROWS, EDGE, EDGE), jnp.float32),
             pltpu.SemaphoreType.DMA((ROWS, SLOTS)),
@@ -300,9 +300,9 @@
             pltpu.SemaphoreType.DMA((ROWS,)),
             pltpu.SemaphoreType.DMA((ROWS,)),
         ],
-        compiler_params=pltpu.CompilerParams(vmem_limit_bytes=VMEM_LIMIT),
+        compiler_params=pltpu.CompilerParams(vmem_limit_bytes=SQUARE_VMEM),
         name="update_rows",
-    )(table, *in_hbm(left_a + left_b + right))
+    )(table, *in_hbm(left_a + left_b), staged, *in_hbm(right))
 
 
 def _mod4(v):
@@ -462,10 +462,10 @@
     haa = move(after(ha, gwa, gwb), MOVE_XA, "haa")
     hwa = move(hw, MOVE_XA, "hwa")
     hwb = move(hw, MOVE_XB, "hwb")
+    staged = stage_rows([square_a, ga, gb, gw, gwa, gwb, gaa, gwaa])
     hwaa = move(haa, MOVE_YP, "hwaa")
-    panel = [square_a, ga, gb, gw, gwa, gwb, gaa, gwaa]
-    panel += [square_b, ha, hb, hw, hwa, hwb, haa, hwaa]
-    square, update = update_rows(second_table, left_a, left_b, panel, scale)
+    panel_b = [square_b, ha, hb, hw, hwa, hwb, haa, hwaa]
+    square, update, _ = update_rows(second_table, left_a, left_b, staged, panel_b, scale)
     return square[:, None], update[:, None]
 
 

time: 224 us -> 222 us (level)
  waiting for transfers between devices: 115 us -> 109 us
  starting transfers between devices: 59 us -> 62.8 us
    ppermute x53, waiting for transfers between devices: 115 us -> 109 us  [move(): return lax.ppermute(value, AXES, moves)]
    ppermute x53, starting transfers between devices: 59 us -> 62.8 us  [move(): return lax.ppermute(value, AXES, moves)]
    pallas_call x1 -> x2, Pallas kernels: 3.47 us -> 5.69 us  [stage_rows(): pl.pallas_call(_stage_kernel, out_shape=pltpu.VMEM((ATOMS + 1, EDGE, EDGE...]
    unnamed x90 -> x88, local copies, waits for them, and re-layouts: 5.91 us -> 7.22 us
  transfers between devices with their start and end apart: 53 -> 53, of which waited for: 18 -> 17; matrix products, arithmetic and copies ran while one was open for 4% -> 3% of each run, Pallas kernels for 9% -> 9%
where the time goes in v3:
time: 222 us
  waiting for transfers between devices  109 us (49%)
  starting transfers between devices  62.8 us (28%)
  Pallas kernels  33.4 us (15%)
  local copies, waits for them, and re-layouts  8.44 us (4%)
  other arithmetic  6.21 us (3%)
    ppermute x53, waiting for transfers between devices, move(): return lax.ppermute(value, AXES, moves)  109 us
    ppermute x53, starting transfers between devices, move(): return lax.ppermute(value, AXES, moves)  62.8 us
    pallas_call x1, Pallas kernels, update_rows(): pl.pallas_call(lambda *refs: _update_kernel(scale, *refs), out_shape=(out...  12.6 us
    pallas_call x2, Pallas kernels, square_rows(): pl.pallas_call(lambda *refs: _square_kernel(scale, n_rows, *refs), out_sh...  11.8 us
    unnamed x88, local copies, waits for them, and re-layouts  7.22 us
    pallas_call x2, Pallas kernels, stage_rows(): pl.pallas_call(_stage_kernel, out_shape=pltpu.VMEM((ATOMS + 1, EDGE, EDGE...  5.69 us
  transfers between devices with their start and end apart: 53, of which 17 were waited for; matrix products, arithmetic and copies ran while one was open for 3% of the time, Pallas kernels for 9%

profile of v3, /device:TPU:1, one launch (start us, length us, event | category | flops | bytes accessed | tf_op | source)
XLA Modules:
  0.0 221.6 jit_solution(15444211392967138078)
XLA Ops:
  0.6 2.2 collective-permute-start.2
  6.7 22.6 %collective-permute-done.refs_1_ = f32[16,128,128]{2,1,0:T(8,128)} collective-permute-done((f32[16,128,128]{2,1,0:T(8,128)}, f32[16,128,128]{2,1,0:T(8,128)}, u32[]{:S(2)}, u32[]{:S(2)}) %collective-permute-start) | collective-permute-done | bytes 1048608 | tf_op jit(solution)/shard_map/a/ppermute | solution.py:56
  37.6 3.8 %collective-permute-start.3 = (f32[8,128,128]{2,1,0:T(8,128)S(1)}, f32[8,128,128]{2,1,0:T(8,128)}, u32[]{:S(2)}, u32[]{:S(2)}) collective-permute-start(f32[8,128,128]{2,1,0:T(8,128)S(1)} %pick_rows.2.refs_1_), channel_id=1, source_target_pairs={{0,4},{1,13},{2,6},{3,15},{4,8},{5,1},{6,10},{7,3},{8,12},{9,5},{1... | collective-permute-start | bytes 1572872 | tf_op jit(solution)/shard_map/fa/ppermute | solution.py:56
  41.3 2.7 %collective-permute-start.11 = (f32[16,128,128]{2,1,0:T(8,128)S(1)}, f32[16,128,128]{2,1,0:T(8,128)}, u32[]{:S(2)}, u32[]{:S(2)}) collective-permute-start(f32[16,128,128]{2,1,0:T(8,128)S(1)} %collective-permute-done.2.refs_3_), channel_id=1, source_target_pairs={{0,32},{1,97},{2,34},{3,99},{4,36},{5,101},{6,38},{7,103},{8,40},{... | collective-permute-start | bytes 3145736 | tf_op jit(solution)/shard_map/wa/ppermute | solution.py:56
  50.9 8.1 %collective-permute-done.6.refs_4_ = f32[8,128,128]{2,1,0:T(8,128)} collective-permute-done((f32[8,128,128]{2,1,0:T(8,128)}, f32[8,128,128]{2,1,0:T(8,128)}, u32[]{:S(2)}, u32[]{:S(2)}) %collective-permute-start.6) | collective-permute-done | bytes 524320 | tf_op jit(solution)/shard_map/fh/ppermute | solution.py:56
  59.0 3.2 %collective-permute-start.15 = (f32[8,128,128]{2,1,0:T(8,128)S(1)}, f32[8,128,128]{2,1,0:T(8,128)}, u32[]{:S(2)}, u32[]{:S(2)}) collective-permute-start(f32[8,128,128]{2,1,0:T(8,128)S(1)} %pick_rows.2.refs_1_), channel_id=1, source_target_pairs={{0,1},{1,0},{2,3},{3,2},{4,5},{5,4},{6,7},{7,6},{8,9},{9,8},{10,11... | collective-permute-start | bytes 1572872 | tf_op jit(solution)/shard_map/fc/ppermute | solution.py:56
  62.2 5.7 %collective-permute-done.12.refs_1_.refs_5_ = f32[16,128,128]{2,1,0:T(8,128)} collective-permute-done((f32[16,128,128]{2,1,0:T(8,128)S(1)}, f32[16,128,128]{2,1,0:T(8,128)}, u32[]{:S(2)}, u32[]{:S(2)}) %collective-permute-start.12) | collective-permute-done | bytes 1048608 | tf_op jit(solution)/shard_map/wb/ppermute | solution.py:56
  71.0 7.6 %collective-permute-done.13.refs_3_.refs_7_ = f32[16,128,128]{2,1,0:T(8,128)} collective-permute-done((f32[16,128,128]{2,1,0:T(8,128)}, f32[16,128,128]{2,1,0:T(8,128)}, u32[]{:S(2)}, u32[]{:S(2)}) %collective-permute-start.13) | collective-permute-done | bytes 1048608 | tf_op jit(solution)/shard_map/waa/ppermute | solution.py:56
  80.7 3.6 %collective-permute-start.18 = (f32[8,128,128]{2,1,0:T(8,128)}, f32[8,128,128]{2,1,0:T(8,128)S(1)}, u32[]{:S(2)}, u32[]{:S(2)}) collective-permute-start(f32[8,128,128]{2,1,0:T(8,128)} %collective-permute-done.6.refs_4_), channel_id=1, source_target_pairs={{0,1},{1,0},{2,3},{3,2},{4,5},{5,4},{6,7},{7,6},{8,9},{9,8},{10,11... | collective-permute-start | bytes 1572872 | tf_op jit(solution)/shard_map/fch/ppermute | solution.py:56
  86.0 5.8 %collective-permute-done.9.refs_6_ = f32[8,128,128]{2,1,0:T(8,128)S(1)} collective-permute-done((f32[8,128,128]{2,1,0:T(8,128)}, f32[8,128,128]{2,1,0:T(8,128)S(1)}, u32[]{:S(2)}, u32[]{:S(2)}) %collective-permute-start.9) | collective-permute-done | bytes 524320 | tf_op jit(solution)/shard_map/fhb/ppermute | solution.py:56
  91.7 5.2 %collective-permute-start.20 = (f32[8,128,128]{2,1,0:T(8,128)S(1)}, f32[8,128,128]{2,1,0:T(8,128)S(1)}, u32[]{:S(2)}, u32[]{:S(2)}) collective-permute-start(f32[8,128,128]{2,1,0:T(8,128)S(1)} %collective-permute-done.9.refs_6_), channel_id=1, source_target_pairs={{0,1},{1,0},{2,3},{3,2},{4,5},{5,4},{6,7},{7,6},{8,9},{9,8},{10,11... | collective-permute-start | bytes 1572872 | tf_op jit(solution)/shard_map/fchb/ppermute | solution.py:56
  98.4 3.5 %stage_rows.2.refs_17_ = f32[129,128,128]{2,1,0:T(8,128)S(1)} custom-call(f32[16,128,128]{2,1,0:T(8,128)} %bitcast.16, f32[16,128,128]{2,1,0:T(8,128)} %collective-permute-done.refs_1_, f32[16,128,128]{2,1,0:T(8,128)} %copy-done.4, f32[16,128,128]{2,1,0:T(8,128)} %copy-done.3, f32[16,128,128]{2,1,0:T(8,128)} %collective-permute-done.11.refs_0_.refs_4_, ...), custom_call_target="tpu_custom_call" | custom-call | tf_op jit(solution)/shard_map/stage_rows/pallas_call | solution.py:177
  102.0 2.9 %collective-permute-start.23 = (f32[8,128,128]{2,1,0:T(8,128)S(1)}, f32[8,128,128]{2,1,0:T(8,128)S(1)}, u32[]{:S(2)}, u32[]{:S(2)}) collective-permute-start(f32[8,128,128]{2,1,0:T(8,128)S(1)} %pick_rows.3.refs_1_.refs_17_), channel_id=1, source_target_pairs={{0,4},{1,13},{2,6},{3,15},{4,8},{5,1},{6,10},{7,3},{8,12},{9,5},{1... | collective-permute-start | bytes 1572872 | tf_op jit(solution)/shard_map/sa/ppermute | solution.py:56
  106.7 6.5 %square_rows.2.refs_0_ = f32[8,128,128]{2,1,0:T(8,128)S(1)} custom-call(s32[8,64]{1,0:T(8,128)S(1)} %get-tuple-element.22.refs_0_, f32[8,128,128]{2,1,0:T(8,128)} %copy-done, f32[8,128,128]{2,1,0:T(8,128)} %collective-permute-done.3.refs_2_, f32[8,128,128]{2,1,0:T(8,128)} %collective-permute-done.4.refs_3_, f32[8,128,128]{2,1,0:T(8,128)} %collective-permute-done.6.refs_4_, ...), custom_call_target="tpu_custom_call" | custom-call | tf_op jit(solution)/shard_map/square_rows/pallas_call | solution.py:214
  113.2 2.5 %collective-permute-start.33 = (f32[8,128,128]{2,1,0:T(8,128)S(1)}, f32[8,128,128]{2,1,0:T(8,128)S(1)}, u32[]{:S(2)}, u32[]{:S(2)}) collective-permute-start(f32[8,128,128]{2,1,0:T(8,128)S(1)} %square_rows.2.refs_0_), channel_id=1, source_target_pairs={{0,32},{1,97},{2,34},{3,99},{4,36},{5,101},{6,38},{7,103},{8,40},{... | collective-permute-start | bytes 1572872 | tf_op jit(solution)/shard_map/ga/ppermute | solution.py:56
  117.3 10.0 %collective-permute-done.33.refs_1_ = f32[8,128,128]{2,1,0:T(8,128)S(1)} collective-permute-done((f32[8,128,128]{2,1,0:T(8,128)S(1)}, f32[8,128,128]{2,1,0:T(8,128)S(1)}, u32[]{:S(2)}, u32[]{:S(2)}) %collective-permute-start.33) | collective-permute-done | bytes 524320 | tf_op jit(solution)/shard_map/ga/ppermute | solution.py:56
  127.3 3.4 %collective-permute-start.34 = (f32[8,128,128]{2,1,0:T(8,128)S(1)}, f32[8,128,128]{2,1,0:T(8,128)S(1)}, u32[]{:S(2)}, u32[]{:S(2)}) collective-permute-start(f32[8,128,128]{2,1,0:T(8,128)S(1)} %collective-permute-done.33.refs_1_), channel_id=1, source_target_pairs={{0,32},{1,97},{2,34},{3,99},{4,36},{5,101},{6,38},{7,103},{8,40},{... | collective-permute-start | bytes 1572872 | tf_op jit(solution)/shard_map/gaa/ppermute | solution.py:56
  131.6 3.5 %collective-permute-done.28.refs_3_ = f32[8,128,128]{2,1,0:T(8,128)S(1)} collective-permute-done((f32[8,128,128]{2,1,0:T(8,128)S(1)}, f32[8,128,128]{2,1,0:T(8,128)S(1)}, u32[]{:S(2)}, u32[]{:S(2)}) %collective-permute-start.28) | collective-permute-done | bytes 524320 | tf_op jit(solution)/shard_map/gw/ppermute | solution.py:56
  137.7 8.4 %collective-permute-done.30.refs_5_.refs_21_ = f32[8,128,128]{2,1,0:T(8,128)S(1)} collective-permute-done((f32[8,128,128]{2,1,0:T(8,128)S(1)}, f32[8,128,128]{2,1,0:T(8,128)S(1)}, u32[]{:S(2)}, u32[]{:S(2)}) %collective-permute-start.30) | collective-permute-done | bytes 524320 | tf_op jit(solution)/shard_map/sha/ppermute | solution.py:56
  147.2 7.4 %collective-permute-done.32.refs_7_.refs_23_ = f32[8,128,128]{2,1,0:T(8,128)S(1)} collective-permute-done((f32[8,128,128]{2,1,0:T(8,128)S(1)}, f32[8,128,128]{2,1,0:T(8,128)S(1)}, u32[]{:S(2)}, u32[]{:S(2)}) %collective-permute-start.32) | collective-permute-done | bytes 524320 | tf_op jit(solution)/shard_map/saa/ppermute | solution.py:56
  155.2 4.7 %collective-permute-done.35.refs_8_.refs_24_ = f32[8,128,128]{2,1,0:T(8,128)S(1)} collective-permute-done((f32[8,128,128]{2,1,0:T(8,128)S(1)}, f32[8,128,128]{2,1,0:T(8,128)S(1)}, u32[]{:S(2)}, u32[]{:S(2)}) %collective-permute-start.35) | collective-permute-done | bytes 524320 | tf_op jit(solution)/shard_map/shaa/ppermute | solution.py:56
  160.0 2.6 %collective-permute-start.43 = (f32[8,128,128]{2,1,0:T(8,128)S(1)}, f32[8,128,128]{2,1,0:T(8,128)S(1)}, u32[]{:S(2)}, u32[]{:S(2)}) collective-permute-start(f32[8,128,128]{2,1,0:T(8,128)S(1)} %collective-permute-done.28.refs_3_), channel_id=1, source_target_pairs={{0,32},{1,97},{2,34},{3,99},{4,36},{5,101},{6,38},{7,103},{8,40},{... | collective-permute-start | bytes 1572872 | tf_op jit(solution)/shard_map/gwa/ppermute | solution.py:56
  163.8 5.3 %square_rows.3.refs_34_ = f32[8,128,128]{2,1,0:T(8,128)S(1)} custom-call(s32[8,64]{1,0:T(8,128)S(1)} %get-tuple-element.58.refs_0_, f32[8,128,128]{2,1,0:T(8,128)} %copy-done.1, f32[8,128,128]{2,1,0:T(8,128)} %copy-done.16, f32[8,128,128]{2,1,0:T(8,128)} %copy-done.18, f32[8,128,128]{2,1,0:T(8,128)} %copy-done.17, f32[8,128,128]{2,1,0:T(8,128)} %copy-done.19, ...), custom_call_target="tpu_custom_call" | custom-call | tf_op jit(solution)/shard_map/square_rows/pallas_call | solution.py:214
  169.9 2.2 collective-permute-start.48
  173.6 6.1 %collective-permute-done.46.refs_35_ = f32[8,128,128]{2,1,0:T(8,128)S(1)} collective-permute-done((f32[8,128,128]{2,1,0:T(8,128)S(1)}, f32[8,128,128]{2,1,0:T(8,128)S(1)}, u32[]{:S(2)}, u32[]{:S(2)}) %collective-permute-start.46) | collective-permute-done | bytes 524320 | tf_op jit(solution)/shard_map/ha/ppermute | solution.py:56
  179.7 2.0 collective-permute-start.51
  184.5 2.4 %collective-permute-start.49 = (f32[8,128,128]{2,1,0:T(8,128)S(1)}, f32[8,128,128]{2,1,0:T(8,128)S(1)}, u32[]{:S(2)}, u32[]{:S(2)}) collective-permute-start(f32[8,128,128]{2,1,0:T(8,128)S(1)} %collective-permute-done.48.refs_37_), channel_id=1, source_target_pairs={{0,32},{1,97},{2,34},{3,99},{4,36},{5,101},{6,38},{7,103},{8,40},{... | collective-permute-start | bytes 1572872 | tf_op jit(solution)/shard_map/hwa/ppermute | solution.py:56
  187.0 3.7 %collective-permute-done.51.refs_40_ = f32[8,128,128]{2,1,0:T(8,128)S(1)} collective-permute-done((f32[8,128,128]{2,1,0:T(8,128)S(1)}, f32[8,128,128]{2,1,0:T(8,128)S(1)}, u32[]{:S(2)}, u32[]{:S(2)}) %collective-permute-start.51) | collective-permute-done | bytes 524320 | tf_op jit(solution)/shard_map/haa/ppermute | solution.py:56
  192.7 3.1 %collective-permute-done.45.refs_7_ = f32[8,128,128]{2,1,0:T(8,128)S(1)} collective-permute-done((f32[8,128,128]{2,1,0:T(8,128)S(1)}, f32[8,128,128]{2,1,0:T(8,128)S(1)}, u32[]{:S(2)}, u32[]{:S(2)}) %collective-permute-start.45) | collective-permute-done | bytes 524320 | tf_op jit(solution)/shard_map/gwaa/ppermute | solution.py:56
  196.6 2.2 stage_rows.3.refs_33_
  198.9 8.8 %collective-permute-done.50.refs_39_ = f32[8,128,128]{2,1,0:T(8,128)S(1)} collective-permute-done((f32[8,128,128]{2,1,0:T(8,128)S(1)}, f32[8,128,128]{2,1,0:T(8,128)S(1)}, u32[]{:S(2)}, u32[]{:S(2)}) %collective-permute-start.50) | collective-permute-done | bytes 524320 | tf_op jit(solution)/shard_map/hwb/ppermute | solution.py:56
  208.9 12.6 %update_rows.1 = (f32[16,128,128]{2,1,0:T(8,128)}, f32[16,128,128]{2,1,0:T(8,128)}, f32[129,128,128]{2,1,0:T(8,128)S(1)}) custom-call(s32[16,64]{1,0:T(8,128)S(1)} %get-tuple-element.57.refs_0_, f32[8,128,128]{2,1,0:T(8,128)} %copy-done, f32[8,128,128]{2,1,0:T(8,128)} %collective-permute-done.3.refs_2_, ...), custom_call_target="tpu_custom_call", output_to_operand_aliasing={{2}: (33, {})} | custom-call | tf_op jit(solution)/shard_map/update_rows/pallas_call | solution.py:288
  (207 shorter events, 46.0 us)
Async XLA Ops:
  0.6 31.6 %collective-permute-start.2 = (f32[16,128,128]{2,1,0:T(8,128)}, f32[16,128,128]{2,1,0:T(8,128)S(1)}, u32[]{:S(2)}, u32[]{:S(2)}) collective-permute-start(f32[16,128,128]{2,1,0:T(8,128)} %bitcast.13), channel_id=1, source_target_pairs={{0,16},{1,17},{2,18},{3,19},{4,20},{5,21},{6,22},{7,23},{8,24},{9,... | collective-permute-start | bytes 3145736 | tf_op jit(solution)/shard_map/w/ppermute | solution.py:56
  2.8 29.5 %collective-permute-start.1 = (f32[16,128,128]{2,1,0:T(8,128)}, f32[16,128,128]{2,1,0:T(8,128)S(1)}, u32[]{:S(2)}, u32[]{:S(2)}) collective-permute-start(f32[16,128,128]{2,1,0:T(8,128)} %bitcast.14), channel_id=1, source_target_pairs={{0,96},{1,33},{2,98},{3,35},{4,100},{5,37},{6,102},{7,39},{8,104},... | collective-permute-start | bytes 3145736 | tf_op jit(solution)/shard_map/b/ppermute | solution.py:56
  4.0 25.3 %collective-permute-start = (f32[16,128,128]{2,1,0:T(8,128)}, f32[16,128,128]{2,1,0:T(8,128)}, u32[]{:S(2)}, u32[]{:S(2)}) collective-permute-start(f32[16,128,128]{2,1,0:T(8,128)} %bitcast.15), channel_id=1, source_target_pairs={{0,32},{1,97},{2,34},{3,99},{4,36},{5,101},{6,38},{7,103},{8,40},{... | collective-permute-start | bytes 3145736 | tf_op jit(solution)/shard_map/a/ppermute | solution.py:56
  29.3 19.5 %collective-permute-start.7 = (f32[16,128,128]{2,1,0:T(8,128)}, f32[16,128,128]{2,1,0:T(8,128)}, u32[]{:S(2)}, u32[]{:S(2)}) collective-permute-start(f32[16,128,128]{2,1,0:T(8,128)} %collective-permute-done.refs_1_), channel_id=1, source_target_pairs={{0,32},{1,97},{2,34},{3,99},{4,36},{5,101},{6,38},{7,103},{8,40},{... | collective-permute-start | bytes 3145736 | tf_op jit(solution)/shard_map/aa/ppermute | solution.py:56
  41.3 26.6 %collective-permute-start.12 = (f32[16,128,128]{2,1,0:T(8,128)S(1)}, f32[16,128,128]{2,1,0:T(8,128)}, u32[]{:S(2)}, u32[]{:S(2)}) collective-permute-start(f32[16,128,128]{2,1,0:T(8,128)S(1)} %collective-permute-done.2.refs_3_), channel_id=1, source_target_pairs={{0,96},{1,33},{2,98},{3,35},{4,100},{5,37},{6,102},{7,39},{8,104},... | collective-permute-start | bytes 3145736 | tf_op jit(solution)/shard_map/wb/ppermute | solution.py:56
  41.3 26.6 %collective-permute-start.11 = (f32[16,128,128]{2,1,0:T(8,128)S(1)}, f32[16,128,128]{2,1,0:T(8,128)}, u32[]{:S(2)}, u32[]{:S(2)}) collective-permute-start(f32[16,128,128]{2,1,0:T(8,128)S(1)} %collective-permute-done.2.refs_3_), channel_id=1, source_target_pairs={{0,32},{1,97},{2,34},{3,99},{4,36},{5,101},{6,38},{7,103},{8,40},{... | collective-permute-start | bytes 3145736 | tf_op jit(solution)/shard_map/wa/ppermute | solution.py:56
  44.6 17.5 %collective-permute-start.4 = (f32[8,128,128]{2,1,0:T(8,128)S(1)}, f32[8,128,128]{2,1,0:T(8,128)}, u32[]{:S(2)}, u32[]{:S(2)}) collective-permute-start(f32[8,128,128]{2,1,0:T(8,128)S(1)} %pick_rows.2.refs_1_), channel_id=1, source_target_pairs={{0,12},{1,5},{2,14},{3,7},{4,0},{5,9},{6,2},{7,11},{8,4},{9,13},{1... | collective-permute-start | bytes 1572872 | tf_op jit(solution)/shard_map/fb/ppermute | solution.py:56
  48.8 29.7 %collective-permute-start.13 = (f32[16,128,128]{2,1,0:T(8,128)}, f32[16,128,128]{2,1,0:T(8,128)}, u32[]{:S(2)}, u32[]{:S(2)}) collective-permute-start(f32[16,128,128]{2,1,0:T(8,128)} %collective-permute-done.7.refs_2_.refs_6_), channel_id=1, source_target_pairs={{0,16},{1,17},{2,18},{3,19},{4,20},{5,21},{6,22},{7,23},{8,24},{9,... | collective-permute-start | bytes 3145736 | tf_op jit(solution)/shard_map/waa/ppermute | solution.py:56
  59.0 21.7 %collective-permute-start.15 = (f32[8,128,128]{2,1,0:T(8,128)S(1)}, f32[8,128,128]{2,1,0:T(8,128)}, u32[]{:S(2)}, u32[]{:S(2)}) collective-permute-start(f32[8,128,128]{2,1,0:T(8,128)S(1)} %pick_rows.2.refs_1_), channel_id=1, source_target_pairs={{0,1},{1,0},{2,3},{3,2},{4,5},{5,4},{6,7},{7,6},{8,9},{9,8},{10,11... | collective-permute-start | bytes 1572872 | tf_op jit(solution)/shard_map/fc/ppermute | solution.py:56
  62.1 22.3 %collective-permute-start.10 = (f32[8,128,128]{2,1,0:T(8,128)}, f32[8,128,128]{2,1,0:T(8,128)}, u32[]{:S(2)}, u32[]{:S(2)}) collective-permute-start(f32[8,128,128]{2,1,0:T(8,128)} %collective-permute-done.3.refs_2_), channel_id=1, source_target_pairs={{0,4},{1,13},{2,6},{3,15},{4,8},{5,1},{6,10},{7,3},{8,12},{9,5},{1... | collective-permute-start | bytes 1572872 | tf_op jit(solution)/shard_map/faa/ppermute | solution.py:56
  67.9 16.5 %collective-permute-start.17 = (f32[8,128,128]{2,1,0:T(8,128)}, f32[8,128,128]{2,1,0:T(8,128)}, u32[]{:S(2)}, u32[]{:S(2)}) collective-permute-start(f32[8,128,128]{2,1,0:T(8,128)} %collective-permute-done.4.refs_3_), channel_id=1, source_target_pairs={{0,1},{1,0},{2,3},{3,2},{4,5},{5,4},{6,7},{7,6},{8,9},{9,8},{10,11... | collective-permute-start | bytes 1572872 | tf_op jit(solution)/shard_map/fcb/ppermute | solution.py:56
  80.7 16.2 %collective-permute-start.18 = (f32[8,128,128]{2,1,0:T(8,128)}, f32[8,128,128]{2,1,0:T(8,128)S(1)}, u32[]{:S(2)}, u32[]{:S(2)}) collective-permute-start(f32[8,128,128]{2,1,0:T(8,128)} %collective-permute-done.6.refs_4_), channel_id=1, source_target_pairs={{0,1},{1,0},{2,3},{3,2},{4,5},{5,4},{6,7},{7,6},{8,9},{9,8},{10,11... | collective-permute-start | bytes 1572872 | tf_op jit(solution)/shard_map/fch/ppermute | solution.py:56
  85.4 16.5 %collective-permute-start.21 = (f32[8,128,128]{2,1,0:T(8,128)}, f32[8,128,128]{2,1,0:T(8,128)S(1)}, u32[]{:S(2)}, u32[]{:S(2)}) collective-permute-start(f32[8,128,128]{2,1,0:T(8,128)} %collective-permute-done.10.refs_7_), channel_id=1, source_target_pairs={{0,1},{1,0},{2,3},{3,2},{4,5},{5,4},{6,7},{7,6},{8,9},{9,8},{10,11... | collective-permute-start | bytes 1572872 | tf_op jit(solution)/shard_map/fcaa/ppermute | solution.py:56
  97.0 18.8 %collective-permute-start.25 = (f32[8,128,128]{2,1,0:T(8,128)S(1)}, f32[8,128,128]{2,1,0:T(8,128)S(1)}, u32[]{:S(2)}, u32[]{:S(2)}) collective-permute-start(f32[8,128,128]{2,1,0:T(8,128)S(1)} %pick_rows.3.refs_1_.refs_17_), channel_id=1, source_target_pairs={{0,16},{1,19},{2,18},{3,17},{4,20},{5,23},{6,22},{7,21},{8,24},{9,... | collective-permute-start | bytes 1572872 | tf_op jit(solution)/shard_map/sy/ppermute | solution.py:56
  102.0 15.2 %collective-permute-start.23 = (f32[8,128,128]{2,1,0:T(8,128)S(1)}, f32[8,128,128]{2,1,0:T(8,128)S(1)}, u32[]{:S(2)}, u32[]{:S(2)}) collective-permute-start(f32[8,128,128]{2,1,0:T(8,128)S(1)} %pick_rows.3.refs_1_.refs_17_), channel_id=1, source_target_pairs={{0,4},{1,13},{2,6},{3,15},{4,8},{5,1},{6,10},{7,3},{8,12},{9,5},{1... | collective-permute-start | bytes 1572872 | tf_op jit(solution)/shard_map/sa/ppermute | solution.py:56
  113.2 14.1 %collective-permute-start.33 = (f32[8,128,128]{2,1,0:T(8,128)S(1)}, f32[8,128,128]{2,1,0:T(8,128)S(1)}, u32[]{:S(2)}, u32[]{:S(2)}) collective-permute-start(f32[8,128,128]{2,1,0:T(8,128)S(1)} %square_rows.2.refs_0_), channel_id=1, source_target_pairs={{0,32},{1,97},{2,34},{3,99},{4,36},{5,101},{6,38},{7,103},{8,40},{... | collective-permute-start | bytes 1572872 | tf_op jit(solution)/shard_map/ga/ppermute | solution.py:56
  115.7 15.0 %collective-permute-start.27 = (f32[8,128,128]{2,1,0:T(8,128)S(1)}, f32[8,128,128]{2,1,0:T(8,128)S(1)}, u32[]{:S(2)}, u32[]{:S(2)}) collective-permute-start(f32[8,128,128]{2,1,0:T(8,128)S(1)} %collective-permute-done.25), channel_id=1, source_target_pairs={{0,16},{1,19},{2,18},{3,17},{4,20},{5,23},{6,22},{7,21},{8,24},{9,... | collective-permute-start | bytes 1572872 | tf_op jit(solution)/shard_map/sh/ppermute | solution.py:56
  116.8 13.9 %collective-permute-start.29 = (f32[8,128,128]{2,1,0:T(8,128)S(1)}, f32[8,128,128]{2,1,0:T(8,128)S(1)}, u32[]{:S(2)}, u32[]{:S(2)}) collective-permute-start(f32[8,128,128]{2,1,0:T(8,128)S(1)} %square_rows.2.refs_0_), channel_id=1, source_target_pairs={{0,96},{1,33},{2,98},{3,35},{4,100},{5,37},{6,102},{7,39},{8,104},... | collective-permute-start | bytes 1572872 | tf_op jit(solution)/shard_map/gb/ppermute | solution.py:56
  116.8 18.2 %collective-permute-start.28 = (f32[8,128,128]{2,1,0:T(8,128)S(1)}, f32[8,128,128]{2,1,0:T(8,128)S(1)}, u32[]{:S(2)}, u32[]{:S(2)}) collective-permute-start(f32[8,128,128]{2,1,0:T(8,128)S(1)} %square_rows.2.refs_0_), channel_id=1, source_target_pairs={{0,16},{1,17},{2,18},{3,19},{4,20},{5,21},{6,22},{7,23},{8,24},{9,... | collective-permute-start | bytes 1572872 | tf_op jit(solution)/shard_map/gw/ppermute | solution.py:56
  117.2 19.0 %collective-permute-start.24 = (f32[8,128,128]{2,1,0:T(8,128)S(1)}, f32[8,128,128]{2,1,0:T(8,128)S(1)}, u32[]{:S(2)}, u32[]{:S(2)}) collective-permute-start(f32[8,128,128]{2,1,0:T(8,128)S(1)} %pick_rows.3.refs_1_.refs_17_), channel_id=1, source_target_pairs={{0,12},{1,5},{2,14},{3,7},{4,0},{5,9},{6,2},{7,11},{8,4},{9,13},{1... | collective-permute-start | bytes 1572872 | tf_op jit(solution)/shard_map/sb/ppermute | solution.py:56
  136.1 18.4 %collective-permute-start.32 = (f32[8,128,128]{2,1,0:T(8,128)S(1)}, f32[8,128,128]{2,1,0:T(8,128)S(1)}, u32[]{:S(2)}, u32[]{:S(2)}) collective-permute-start(f32[8,128,128]{2,1,0:T(8,128)S(1)} %collective-permute-done.23.refs_2_.refs_18_), channel_id=1, source_target_pairs={{0,4},{1,13},{2,6},{3,15},{4,8},{5,1},{6,10},{7,3},{8,12},{9,5},{1... | collective-permute-start | bytes 1572872 | tf_op jit(solution)/shard_map/saa/ppermute | solution.py:56
  136.2 18.4 %collective-permute-start.37 = (f32[8,128,128]{2,1,0:T(8,128)S(1)}, f32[8,128,128]{2,1,0:T(8,128)S(1)}, u32[]{:S(2)}, u32[]{:S(2)}) collective-permute-start(f32[8,128,128]{2,1,0:T(8,128)S(1)} %collective-permute-done.24.refs_3_.refs_19_), channel_id=1, source_target_pairs={{0,1},{1,0},{2,3},{3,2},{4,5},{5,4},{6,7},{7,6},{8,9},{9,8},{10,11... | collective-permute-start | bytes 1572872 | tf_op jit(solution)/shard_map/scb/ppermute | solution.py:56
  137.3 17.8 %collective-permute-start.31 = (f32[8,128,128]{2,1,0:T(8,128)S(1)}, f32[8,128,128]{2,1,0:T(8,128)S(1)}, u32[]{:S(2)}, u32[]{:S(2)}) collective-permute-start(f32[8,128,128]{2,1,0:T(8,128)S(1)} %collective-permute-done.27.refs_4_.refs_20_), channel_id=1, source_target_pairs={{0,12},{1,5},{2,14},{3,7},{4,0},{5,9},{6,2},{7,11},{8,4},{9,13},{1... | collective-permute-start | bytes 1572872 | tf_op jit(solution)/shard_map/shb/ppermute | solution.py:56
  146.1 13.8 %collective-permute-start.35 = (f32[8,128,128]{2,1,0:T(8,128)S(1)}, f32[8,128,128]{2,1,0:T(8,128)S(1)}, u32[]{:S(2)}, u32[]{:S(2)}) collective-permute-start(f32[8,128,128]{2,1,0:T(8,128)S(1)} %collective-permute-done.30.refs_5_.refs_21_), channel_id=1, source_target_pairs={{0,4},{1,13},{2,6},{3,15},{4,8},{5,1},{6,10},{7,3},{8,12},{9,5},{1... | collective-permute-start | bytes 1572872 | tf_op jit(solution)/shard_map/shaa/ppermute | solution.py:56
  159.9 13.6 %collective-permute-start.44 = (f32[8,128,128]{2,1,0:T(8,128)S(1)}, f32[8,128,128]{2,1,0:T(8,128)S(1)}, u32[]{:S(2)}, u32[]{:S(2)}) collective-permute-start(f32[8,128,128]{2,1,0:T(8,128)S(1)} %collective-permute-done.28.refs_3_), channel_id=1, source_target_pairs={{0,96},{1,33},{2,98},{3,35},{4,100},{5,37},{6,102},{7,39},{8,104},... | collective-permute-start | bytes 1572872 | tf_op jit(solution)/shard_map/gwb/ppermute | solution.py:56
  160.0 13.6 %collective-permute-start.43 = (f32[8,128,128]{2,1,0:T(8,128)S(1)}, f32[8,128,128]{2,1,0:T(8,128)S(1)}, u32[]{:S(2)}, u32[]{:S(2)}) collective-permute-start(f32[8,128,128]{2,1,0:T(8,128)S(1)} %collective-permute-done.28.refs_3_), channel_id=1, source_target_pairs={{0,32},{1,97},{2,34},{3,99},{4,36},{5,101},{6,38},{7,103},{8,40},{... | collective-permute-start | bytes 1572872 | tf_op jit(solution)/shard_map/gwa/ppermute | solution.py:56
  169.9 14.4 %collective-permute-start.48 = (f32[8,128,128]{2,1,0:T(8,128)S(1)}, f32[8,128,128]{2,1,0:T(8,128)S(1)}, u32[]{:S(2)}, u32[]{:S(2)}) collective-permute-start(f32[8,128,128]{2,1,0:T(8,128)S(1)} %square_rows.3.refs_34_), channel_id=1, source_target_pairs={{0,16},{1,17},{2,18},{3,19},{4,20},{5,21},{6,22},{7,23},{8,24},{9,... | collective-permute-start | bytes 1572872 | tf_op jit(solution)/shard_map/hw/ppermute | solution.py:56
  181.7 14.1 %collective-permute-start.45 = (f32[8,128,128]{2,1,0:T(8,128)S(1)}, f32[8,128,128]{2,1,0:T(8,128)S(1)}, u32[]{:S(2)}, u32[]{:S(2)}) collective-permute-start(f32[8,128,128]{2,1,0:T(8,128)S(1)} %collective-permute-done.34.refs_6_), channel_id=1, source_target_pairs={{0,16},{1,17},{2,18},{3,19},{4,20},{5,21},{6,22},{7,23},{8,24},{9,... | collective-permute-start | bytes 1572872 | tf_op jit(solution)/shard_map/gwaa/ppermute | solution.py:56
  183.7 15.2 %collective-permute-start.47 = (f32[8,128,128]{2,1,0:T(8,128)S(1)}, f32[8,128,128]{2,1,0:T(8,128)S(1)}, u32[]{:S(2)}, u32[]{:S(2)}) collective-permute-start(f32[8,128,128]{2,1,0:T(8,128)S(1)} %square_rows.3.refs_34_), channel_id=1, source_target_pairs={{0,96},{1,33},{2,98},{3,35},{4,100},{5,37},{6,102},{7,39},{8,104},... | collective-permute-start | bytes 1572872 | tf_op jit(solution)/shard_map/hb/ppermute | solution.py:56
  184.3 23.4 %collective-permute-start.50 = (f32[8,128,128]{2,1,0:T(8,128)S(1)}, f32[8,128,128]{2,1,0:T(8,128)S(1)}, u32[]{:S(2)}, u32[]{:S(2)}) collective-permute-start(f32[8,128,128]{2,1,0:T(8,128)S(1)} %collective-permute-done.48.refs_37_), channel_id=1, source_target_pairs={{0,96},{1,33},{2,98},{3,35},{4,100},{5,37},{6,102},{7,39},{8,104},... | collective-permute-start | bytes 1572872 | tf_op jit(solution)/shard_map/hwb/ppermute | solution.py:56
  184.5 23.2 %collective-permute-start.49 = (f32[8,128,128]{2,1,0:T(8,128)S(1)}, f32[8,128,128]{2,1,0:T(8,128)S(1)}, u32[]{:S(2)}, u32[]{:S(2)}) collective-permute-start(f32[8,128,128]{2,1,0:T(8,128)S(1)} %collective-permute-done.48.refs_37_), channel_id=1, source_target_pairs={{0,32},{1,97},{2,34},{3,99},{4,36},{5,101},{6,38},{7,103},{8,40},{... | collective-permute-start | bytes 1572872 | tf_op jit(solution)/shard_map/hwa/ppermute | solution.py:56
  190.7 17.0 %collective-permute-start.52 = (f32[8,128,128]{2,1,0:T(8,128)S(1)}, f32[8,128,128]{2,1,0:T(8,128)S(1)}, u32[]{:S(2)}, u32[]{:S(2)}) collective-permute-start(f32[8,128,128]{2,1,0:T(8,128)S(1)} %collective-permute-done.51.refs_40_), channel_id=1, source_target_pairs={{0,16},{1,17},{2,18},{3,19},{4,20},{5,21},{6,22},{7,23},{8,24},{9,... | collective-permute-start | bytes 1572872 | tf_op jit(solution)/shard_map/hwaa/ppermute | solution.py:56
  (65 other events, 1023.0 us)
